TPU v7x, 128 devices: a whole 4x4x4 slice. The times are simulated.
128 devices in a mesh: fsdp: 8 (over z, core), ep: 16 (over x, y).
Axes of the slice: x: 4, y: 4, z: 4, core: 2. Of those that a mesh axis runs over, the one named last changes fastest.
Arguments:
- deltas: bfloat16 [16, 7168, 2048], P('ep', 'fsdp')
- sketch_matrix: bfloat16 [2048, 256], replicated, may hold values from -0.125 to 0.125
- owner_of: int32 [16], replicated, may hold values from 0 to 15, as said below
- serving: bfloat16 [32, 7168, 2048], P('ep', 'fsdp'), may hold values from -4 to 4
Outputs:
- updated: bfloat16 [32, 7168, 2048], P('ep', 'fsdp')
Inputs may be any that keep to these rules, and one draw needn't show every extreme that they name: `owner_of`: each of the 16 owners owns at most 2 experts; in every draw some owner owns exactly 2 and some own none.
All inputs are finite; a program needn't handle non-finite values.
Results may differ from a plain program's by a relative error of at most 0.007.
Values may be sent and summed in bfloat16 or wider, within the bound.
No kernel may reach another device: no remote copies, remote signals or barrier semaphores. Data moves between devices by JAX's collectives and lax.ppermute only.
A program may use at most 128 MiB of HBM per device.

v0:
```python
import jax
import jax.numpy as jnp
from jax import lax
from jax.experimental import pallas as pl
from jax.experimental.pallas import tpu as pltpu
from jax.sharding import Mesh, PartitionSpec as P

D = 7168
FF = 2048
RANK = 256
POWER = 2
SLOTS = 2
N_EP = 16
HALF = RANK // 2
GROUP = 8
CHUNK = FF // 8
SPANS = ((0, 256), (256, 256), (512, 384))
EP = ("x", "y")
SWAP = [(0, 1), (1, 0)]
NT = (((1,), (1,)), ((), ()))
F32 = jnp.float32
BF16 = jnp.bfloat16
VM = pl.BlockSpec(memory_space=pltpu.VMEM)
SM = pl.BlockSpec(memory_space=pltpu.SMEM)
ANY = pl.BlockSpec(memory_space=pl.ANY)


def columns(half, j):
    return pl.ds(pl.multiple_of(half * (FF // 2) + j * CHUNK, CHUNK), CHUNK)


def load_rows(a_hbm, a_ref, sems):
    copies = [
        pltpu.make_async_copy(a_hbm.at[pl.ds(s, n)], a_ref.at[pl.ds(s, n)], sems.at[i])
        for i, (s, n) in enumerate(SPANS)
    ]
    for copy in copies:
        copy.start()
    return copies


def power_tiles(c, a_ref, yt_ref, mine_out, other_out):
    for j in range(4):
        tile = jnp.dot(yt_ref[...], a_ref[:, columns(1 - c, j)], preferred_element_type=F32)
        other_out[j] = tile.astype(BF16)
    for j in range(4):
        mine_out[j] = jnp.dot(
            yt_ref[...], a_ref[:, columns(c, j)], preferred_element_type=F32
        )


def sketch_rows(c, a_ref, s, n, mine_ref, other_ref):
    y = None
    for half, steps in ((c, mine_ref), (1 - c, other_ref)):
        for j in range(4):
            term = lax.dot_general(
                a_ref[pl.ds(s, n), columns(half, j)], steps[j], NT, preferred_element_type=F32
            )
            y = term if y is None else y + term
    return y


def first_kernel(c_ref, a_hbm, sketch_ref, mine_out, other_out, a_ref, yt_ref, sems):
    c = c_ref[0]
    copies = load_rows(a_hbm, a_ref, sems)
    for copy, (s, n) in zip(copies, SPANS):
        copy.wait()
        y = jnp.dot(a_ref[pl.ds(s, n), :], sketch_ref[...], preferred_element_type=F32)
        yt_ref[:, pl.ds(s, n)] = y.T.astype(BF16)
    power_tiles(c, a_ref, yt_ref, mine_out, other_out)


def power_kernel(c_ref, a_hbm, mine_ref, other_ref, mine_out, other_out, a_ref, yt_ref, sems):
    c = c_ref[0]
    copies = load_rows(a_hbm, a_ref, sems)
    for copy, (s, n) in zip(copies, SPANS):
        copy.wait()
        y = sketch_rows(c, a_ref, s, n, mine_ref, other_ref)
        yt_ref[:, pl.ds(s, n)] = y.T.astype(BF16)
    power_tiles(c, a_ref, yt_ref, mine_out, other_out)


def last_kernel(
    c_ref, a_hbm, mine_ref, other_ref,
    y_out, mine_out, other_out, gram_mine, gram_other, a_ref, yt_ref, sems,
):
    c = c_ref[0]
    copies = load_rows(a_hbm, a_ref, sems)
    for copy, (s, n) in zip(copies, SPANS):
        copy.wait()
        y = sketch_rows(c, a_ref, s, n, mine_ref, other_ref)
        y_out[pl.ds(s, n), :] = y.astype(BF16)
        yt_ref[:, pl.ds(s, n)] = y.T.astype(BF16)
    for half, out in ((1 - c, gram_other), (c, gram_mine)):
        turned = yt_ref[pl.ds(pl.multiple_of(half * HALF, HALF), HALF), :]
        out[...] = jnp.dot(turned, y_out[...], preferred_element_type=F32)
    power_tiles(c, a_ref, yt_ref, mine_out, other_out)


def sweep(kernel, operands, extra, name):
    rows = operands[1].shape[0]
    tiles = (4, RANK, CHUNK)
    outs = extra[:1] + [
        jax.ShapeDtypeStruct(tiles, F32), jax.ShapeDtypeStruct(tiles, BF16)
    ] + extra[1:]
    return pl.pallas_call(
        kernel,
        in_specs=[SM, ANY] + [VM] * (len(operands) - 2),
        out_specs=[VM] * len(outs),
        out_shape=outs,
        scratch_shapes=[
            pltpu.VMEM((rows, FF), BF16),
            pltpu.VMEM((RANK, rows), BF16),
            pltpu.SemaphoreType.DMA((len(SPANS),)),
        ],
        compiler_params=pltpu.CompilerParams(vmem_limit_bytes=24 << 20),
        name=name,
    )(*operands)


def exact_dot(a, b):
    return jnp.dot(a, b, preferred_element_type=F32, precision=lax.Precision.HIGHEST)


def invert(a_ref, cols_ref):
    lane = lax.broadcasted_iota(jnp.int32, (GROUP, HALF), 1)
    sub = lax.broadcasted_iota(jnp.int32, (GROUP, HALF), 0)
    lane_all = lax.broadcasted_iota(jnp.int32, (HALF, HALF), 1)

    def group(g, carry):
        base = pl.multiple_of(g * GROUP, GROUP)
        rows = a_ref[pl.ds(base, GROUP), :]
        turned = rows.T
        for i in range(GROUP):
            cols_ref[i] = jnp.broadcast_to(turned[:, i : i + 1], (HALF, HALF))
        block = [cols_ref[i, pl.ds(base, GROUP), :] for i in range(GROUP)]
        for j in range(GROUP):
            inverse = 1.0 / jnp.broadcast_to(block[j][j : j + 1], (GROUP, HALF))
            new = []
            for i in range(GROUP):
                if i == j:
                    new.append(jnp.where(sub == j, -inverse, block[j] * inverse))
                else:
                    t = jnp.broadcast_to(block[i][j : j + 1], (GROUP, HALF)) * inverse
                    new.append(jnp.where(sub == j, t, block[i] - block[j] * t))
            block = new
        local = lane - base
        rows = jnp.where((local >= 0) & (local < GROUP), jnp.where(local == sub, 1.0, 0.0), -rows)
        solved = block[0] * jnp.broadcast_to(rows[0:1], (GROUP, HALF))
        for i in range(1, GROUP):
            solved = solved + block[i] * jnp.broadcast_to(rows[i : i + 1], (GROUP, HALF))
        here = lane_all - base
        a = jnp.where((here >= 0) & (here < GROUP), 0.0, a_ref[...])
        for i in range(GROUP):
            a = a - cols_ref[i] * jnp.broadcast_to(solved[i : i + 1], (HALF, HALF))
        a_ref[...] = a
        a_ref[pl.ds(base, GROUP), :] = solved
        return carry

    lax.fori_loop(0, HALF // GROUP, group, 0)


def solve_kernel(c_ref, mine_ref, other_ref, cross_ref, out_ref, a_ref, b_ref, cols_ref, gram_ref):
    c = c_ref[0]
    gram_ref[pl.ds(pl.multiple_of(c * HALF, HALF), HALF), :] = mine_ref[...]
    gram_ref[pl.ds(pl.multiple_of((1 - c) * HALF, HALF), HALF), :] = other_ref[...]
    a_ref[...] = gram_ref[:HALF, :HALF]
    invert(a_ref, cols_ref)
    first = -a_ref[...]
    across = gram_ref[:HALF, HALF:]
    step = exact_dot(first, across)
    b_ref[...] = gram_ref[HALF:, HALF:] - exact_dot(across.T, step)
    invert(b_ref, cols_ref)
    top = cross_ref[:HALF]
    low = cross_ref[HALF:]
    low_solved = -exact_dot(b_ref[...], low - exact_dot(step.T, top))
    top_solved = exact_dot(first, top) - exact_dot(step, low_solved)
    top_solved = top_solved.astype(BF16)
    low_solved = low_solved.astype(BF16)
    for e in range(N_EP):
        out_ref[e, :HALF] = top_solved
        out_ref[e, HALF:] = low_solved


def solve(c, gram_mine, gram_other, cross):
    vm = pl.BlockSpec(memory_space=pltpu.VMEM)
    return pl.pallas_call(
        solve_kernel,
        in_specs=[pl.BlockSpec(memory_space=pltpu.SMEM), vm, vm, vm],
        out_specs=vm,
        out_shape=jax.ShapeDtypeStruct((N_EP, RANK, cross.shape[1]), BF16),
        scratch_shapes=[
            pltpu.VMEM((HALF, HALF), F32),
            pltpu.VMEM((HALF, HALF), F32),
            pltpu.VMEM((GROUP, HALF, HALF), F32),
            pltpu.VMEM((RANK, RANK), F32),
        ],
        compiler_params=pltpu.CompilerParams(vmem_limit_bytes=12 << 20),
        name="solve",
    )(c, gram_mine, gram_other, cross)


def chip_sum(mine, other):
    return mine + lax.ppermute(other, "c", SWAP).astype(F32)


def all_sum(mine, other):
    chip = chip_sum(mine, other).astype(BF16)
    pieces = lax.all_to_all(chip, "z", 0, 0, tiled=True)
    step = (jnp.sum(pieces.astype(F32), axis=0) / D).astype(BF16)
    step_mine = lax.all_gather(step, "z", axis=0)
    return step_mine, lax.ppermute(step_mine, "c", SWAP)


def final_kernel(sel_ref, present_ref, c_ref, y_ref, mine_ref, other_ref, serving_ref, out_ref):
    slot = pl.program_id(0)
    c = c_ref[0]
    owned = present_ref[slot] > 0
    for half, solved in ((c, mine_ref), (1 - c, other_ref)):
        for j in range(4):
            update = jnp.dot(y_ref[0], solved[j, 0], preferred_element_type=F32)
            served = serving_ref[0, :, columns(half, j)].astype(F32)
            summed = served + jnp.where(owned, update, 0.0)
            out_ref[0, :, columns(half, j)] = summed.astype(BF16)


def final(sel, present, c, y_all, mine, other, serving):
    slots, rows, cols = serving.shape
    tile = 448
    block = pl.BlockSpec((1, tile, cols), lambda s, r, sel, pr, c: (s, r, 0))
    chunks = pl.BlockSpec((4, 1, RANK, CHUNK), lambda s, r, sel, pr, c: (0, s, 0, 0))
    spec = pltpu.PrefetchScalarGridSpec(
        num_scalar_prefetch=3,
        grid=(slots, rows // tile),
        in_specs=[
            pl.BlockSpec((1, tile, RANK), lambda s, r, sel, pr, c: (sel[s], r, 0)),
            chunks,
            chunks,
            block,
        ],
        out_specs=block,
    )
    return pl.pallas_call(
        final_kernel,
        grid_spec=spec,
        out_shape=jax.ShapeDtypeStruct(serving.shape, BF16),
        compiler_params=pltpu.CompilerParams(
            dimension_semantics=("arbitrary", "arbitrary"), vmem_limit_bytes=32 << 20
        ),
        name="final",
    )(sel, present, c, y_all, mine, other, serving)


def local(deltas, sketch_matrix, owner_of, serving):
    c = lax.axis_index("c").astype(jnp.int32).reshape(1)
    own_index = lax.axis_index("x") * 4 + lax.axis_index("y")
    delta_rows = deltas[0]
    rows = delta_rows.shape[0]
    mine, other = sweep(first_kernel, [c, delta_rows, sketch_matrix], [], "first")
    for iteration in range(POWER - 1):
        step_mine, step_other = all_sum(mine, other)
        mine, other = sweep(power_kernel, [c, delta_rows, step_mine, step_other], [], "power")
    step_mine, step_other = all_sum(mine, other)
    extra = [jax.ShapeDtypeStruct((rows, RANK), BF16)] + [
        jax.ShapeDtypeStruct((HALF, RANK), F32)
    ] * 2
    sketch, mine, other, gram_mine, gram_other = sweep(
        last_kernel, [c, delta_rows, step_mine, step_other], extra, "last"
    )
    y_all = lax.all_gather(sketch, EP, axis=0)

    gram_chip = chip_sum(gram_mine, gram_other)
    gram_hi = lax.reduce_precision(gram_chip, 8, 7)
    gram_lo = (gram_chip - gram_hi).astype(BF16)
    gram_pair = jnp.concatenate([gram_hi.astype(BF16), gram_lo], axis=0)
    cross_chip = chip_sum(mine, other).astype(BF16)
    packed = jnp.concatenate(
        [cross_chip, jnp.broadcast_to(gram_pair[None], (4, RANK, RANK))], axis=1
    )
    pieces = lax.all_to_all(packed, "z", 0, 0, tiled=True)
    sums = jnp.sum(pieces.astype(F32), axis=0)
    cross = sums[:RANK]
    gram_half = sums[RANK : RANK + HALF] + sums[RANK + HALF :]
    solved = solve(c, gram_half, lax.ppermute(gram_half, "c", SWAP), cross)

    is_owned = (owner_of == own_index).astype(jnp.int32)
    owned_rank = jnp.cumsum(is_owned, dtype=jnp.int32) - 1
    slot_ids = jnp.arange(SLOTS, dtype=jnp.int32)
    slot_hits = (is_owned[None, :] == 1) & (owned_rank[None, :] == slot_ids[:, None])
    present = jnp.any(slot_hits, axis=1).astype(jnp.int32)
    expert_ids = jnp.arange(N_EP, dtype=jnp.int32)
    sel = jnp.sum(jnp.where(slot_hits, expert_ids[None, :], 0), axis=1).astype(jnp.int32)

    chunks = lax.all_to_all(solved, EP, 0, 0, tiled=True)
    picked = jnp.stack(
        [lax.dynamic_index_in_dim(chunks, sel[s], 0, keepdims=False) for s in range(SLOTS)]
    )
    solved_mine = lax.all_to_all(
        jnp.broadcast_to(picked[None], (4,) + picked.shape), "z", 0, 0, tiled=True
    )
    solved_other = lax.ppermute(solved_mine, "c", SWAP)
    return final(sel, present, c, y_all, solved_mine, solved_other, serving)


def solution(mesh):
    split = Mesh(mesh.devices.reshape(4, 2, 4, 4), ("z", "c", "x", "y"))
    rows = P(EP, ("z", "c"), None)
    return jax.shard_map(
        local,
        mesh=split,
        in_specs=(rows, P(), P(), rows),
        out_specs=rows,
        check_vma=False,
    )
```

profile of v0, /device:TPU:1, one launch (start us, length us, event | category | flops | bytes accessed | tf_op | source)
XLA Modules:
  0.0 214.3 jit_solution(13668514530843032233)
XLA Ops:
  6.5 2.0 copy-done
  9.8 4.0 %first.1 = (f32[4,256,256]{2,1,0:T(8,128)S(1)}, bf16[4,256,256]{2,1,0:T(8,128)(2,1)S(1)}) custom-call(s32[1]{0:T(128)} %bitcast.1.c_ref, bf16[896,2048]{1,0:T(8,128)(2,1)S(1)} %bitcast.9, bf16[2048,256]{1,0:T(8,128)(2,1)S(1)} %copy-done.3), custom_call_target="tpu_custom_call" | custom-call | tf_op jit(solution)/shard_map/first/pallas_call | solution.py:106
  15.3 1.5 collective-permute-done
  16.9 13.6 %all_to_all.25 = bf16[4,256,256]{2,1,0:T(8,128)(2,1)S(1)} all-to-all(bf16[4,256,256]{2,1,0:T(8,128)(2,1)S(1)} %add_convert_fusion.2), channel_id=1, replica_groups=mesh['z'=4,'c'=2,'x'=4,'y'=4] {'z'}, dimensions={0} | all-to-all | bytes 1048576 | tf_op jit(solution)/shard_map/all_to_all | solution.py:209
  30.6 11.1 %all-gather = bf16[1024,256]{1,0:T(8,128)(2,1)S(1)} all-gather(bf16[256,256]{1,0:T(8,128)(2,1)S(1)} %multiply_convert_fusion.1), channel_id=2, replica_groups=mesh['z'=4,'c'=2,'x'=4,'y'=4] {'z'}, dimensions={0}, use_global_device_ids=true | all-gather | bytes 655360 | tf_op jit(solution)/shard_map/all_gather | solution.py:211
  41.7 3.9 %collective-permute-start.1 = (bf16[4,256,256]{2,1,0:T(8,128)(2,1)S(1)}, bf16[4,256,256]{2,1,0:T(8,128)(2,1)S(1)}, u32[]{:S(2)}, u32[]{:S(2)}) collective-permute-start(bf16[4,256,256]{2,1,0:T(8,128)(2,1)S(1)} %bitcast.15), channel_id=1, source_target_pairs={{0,16},{16,0},{1,17},{17,1},{2,18},{18,2},{3,19},{19,3},{4,20},{20... | collective-permute-start | bytes 1572872 | tf_op jit(solution)/shard_map/ppermute | solution.py:212
  45.6 1.5 collective-permute-done.1.other_ref
  47.2 4.1 %power.1 = (f32[4,256,256]{2,1,0:T(8,128)S(1)}, bf16[4,256,256]{2,1,0:T(8,128)(2,1)S(1)}) custom-call(s32[1]{0:T(128)} %bitcast.1.c_ref, bf16[896,2048]{1,0:T(8,128)(2,1)S(1)} %bitcast.10, bf16[4,256,256]{2,1,0:T(8,128)(2,1)S(1)} %bitcast.16, bf16[4,256,256]{2,1,0:T(8,128)(2,1)S(1)} %collective-permute-done.1.other_ref), custom_call_target="tpu_custom_call" | custom-call | tf_op jit(solution)/shard_map/power/pallas_call | solution.py:106
  53.4 11.5 %all_to_all.26 = bf16[4,256,256]{2,1,0:T(8,128)(2,1)S(1)} all-to-all(bf16[4,256,256]{2,1,0:T(8,128)(2,1)S(1)} %add_convert_fusion.1), channel_id=1, replica_groups=mesh['z'=4,'c'=2,'x'=4,'y'=4] {'z'}, dimensions={0} | all-to-all | bytes 1048576 | tf_op jit(solution)/shard_map/all_to_all | solution.py:209
  65.0 10.5 %all-gather.1 = bf16[1024,256]{1,0:T(8,128)(2,1)S(1)} all-gather(bf16[256,256]{1,0:T(8,128)(2,1)S(1)} %multiply_convert_fusion), channel_id=3, replica_groups=mesh['z'=4,'c'=2,'x'=4,'y'=4] {'z'}, dimensions={0}, use_global_device_ids=true | all-gather | bytes 655360 | tf_op jit(solution)/shard_map/all_gather | solution.py:211
  75.4 4.2 %collective-permute-start.3 = (bf16[4,256,256]{2,1,0:T(8,128)(2,1)S(1)}, bf16[4,256,256]{2,1,0:T(8,128)(2,1)S(1)}, u32[]{:S(2)}, u32[]{:S(2)}) collective-permute-start(bf16[4,256,256]{2,1,0:T(8,128)(2,1)S(1)} %bitcast.13), channel_id=1, source_target_pairs={{0,16},{16,0},{1,17},{17,1},{2,18},{18,2},{3,19},{19,3},{4,20},{20... | collective-permute-start | bytes 1572872 | tf_op jit(solution)/shard_map/ppermute | solution.py:212
  81.2 5.2 %last.1 = (bf16[896,256]{1,0:T(8,128)(2,1)}, f32[4,256,256]{2,1,0:T(8,128)S(1)}, bf16[4,256,256]{2,1,0:T(8,128)(2,1)S(1)}, f32[128,256]{1,0:T(8,128)S(1)}, f32[128,256]{1,0:T(8,128)S(1)}) custom-call(s32[1]{0:T(128)} %bitcast.1.c_ref, bf16[896,2048]{1,0:T(8,128)(2,1)S(1)} %bitcast.11, bf16[4,256,256]{2,1,0:T(8,128)(2,1)S(1)} %bitcast.14, ...), custom_call_target="tpu_custom_call" | custom-call | tf_op jit(solution)/shard_map/last/pallas_call | solution.py:106
  87.0 1.6 collective-permute-done.5
  88.9 17.1 %all_to_all.27 = bf16[4,512,256]{2,1,0:T(8,128)(2,1)S(1)} all-to-all(bf16[4,512,256]{2,1,0:T(8,128)(2,1)S(1)} %pad_maximum_fusion), channel_id=1, replica_groups=mesh['z'=4,'c'=2,'x'=4,'y'=4] {'z'}, dimensions={0} | all-to-all | bytes 2097152 | tf_op jit(solution)/shard_map/all_to_all | solution.py:280
  106.2 1.6 collective-permute-start.6
  108.8 17.7 %solve.1 = bf16[16,256,256]{2,1,0:T(8,128)(2,1)} custom-call(s32[1]{0:T(128)} %bitcast.1.c_ref, f32[128,256]{1,0:T(8,128)S(1)} %slice_add_fusion.mine_ref, f32[128,256]{1,0:T(8,128)S(1)} %collective-permute-done.6.other_ref, f32[256,256]{1,0:T(8,128)S(1)} %slice.22.cross_ref), custom_call_target="tpu_custom_call" | custom-call | tf_op jit(solution)/shard_map/solve/pallas_call | solution.py:187
  126.5 6.9 %all-to-all-start.3 = ((bf16[16,256,256]{2,1,0:T(8,128)(2,1)}), bf16[16,256,256]{2,1,0:T(8,128)(2,1)S(1)}, u32[]{:S(2)}, u32[]{:S(2)}) async-start(bf16[16,256,256]{2,1,0:T(8,128)(2,1)} %solve.1), calls=%async_computation.3 | async-start | bytes 4194304 | tf_op jit(solution)/shard_map/all_to_all | solution.py:294
  138.1 35.7 %all-to-all-done.3 = bf16[16,256,256]{2,1,0:T(8,128)(2,1)S(1)} async-done(((bf16[16,256,256]{2,1,0:T(8,128)(2,1)}), bf16[16,256,256]{2,1,0:T(8,128)(2,1)S(1)}, u32[]{:S(2)}, u32[]{:S(2)}) %all-to-all-start.3) | async-done | bytes 2097184 | tf_op jit(solution)/shard_map/all_to_all | solution.py:294
  173.9 16.9 %all_to_all.28.mine_ref = bf16[4,2,256,256]{3,2,1,0:T(8,128)(2,1)S(1)} all-to-all(bf16[4,2,256,256]{3,2,1,0:T(8,128)(2,1)S(1)} %broadcast_in_dim.19), channel_id=1, replica_groups=mesh['z'=4,'c'=2,'x'=4,'y'=4] {'z'}, dimensions={0} | all-to-all | bytes 2097152 | tf_op jit(solution)/shard_map/all_to_all | solution.py:298
  190.9 2.4 %collective-permute-start.7 = (bf16[4,2,256,256]{3,2,1,0:T(8,128)(2,1)S(1)}, bf16[4,2,256,256]{3,2,1,0:T(8,128)(2,1)S(1)}, u32[]{:S(2)}, u32[]{:S(2)}) collective-permute-start(bf16[4,2,256,256]{3,2,1,0:T(8,128)(2,1)S(1)} %all_to_all.28.mine_ref), channel_id=1, source_target_pairs={{0,16},{16,0},{1,17},{17,1},{2,18},{18,2},{3,19},{19,3},{4,20},{20... | collective-permute-start | bytes 3145736 | tf_op jit(solution)/shard_map/ppermute | solution.py:301
  193.4 2.2 %collective-permute-done.7.other_ref = bf16[4,2,256,256]{3,2,1,0:T(8,128)(2,1)S(1)} collective-permute-done((bf16[4,2,256,256]{3,2,1,0:T(8,128)(2,1)S(1)}, bf16[4,2,256,256]{3,2,1,0:T(8,128)(2,1)S(1)}, u32[]{:S(2)}, u32[]{:S(2)}) %collective-permute-start.7) | collective-permute-done | bytes 1048608 | tf_op jit(solution)/shard_map/ppermute | solution.py:301
  195.6 3.1 %copy-done.1 = bf16[2,896,2048]{2,1,0:T(8,128)(2,1)S(1)} copy-done((bf16[2,896,2048]{2,1,0:T(8,128)(2,1)S(1)}, bf16[2,896,2048]{2,1,0:T(8,128)(2,1)}, u32[]{:S(2)}) %copy-start.1) | copy-done | bytes 7340056
  198.7 3.1 %copy-done.2 = bf16[14336,256]{1,0:T(8,128)(2,1)S(1)} copy-done((bf16[14336,256]{1,0:T(8,128)(2,1)S(1)}, bf16[14336,256]{1,0:T(8,128)(2,1)}, u32[]{:S(2)}) %copy-start.2) | copy-done | bytes 7340056
  201.8 5.7 %final.1 = bf16[2,896,2048]{2,1,0:T(8,128)(2,1)} custom-call(s32[2]{0:T(128)S(1)} %select_reduce_fusion.sel_ref, s32[2]{0:T(128)S(1)} %convert_element_type.66.present_ref, s32[1]{0:T(128)} %bitcast.1.c_ref, bf16[16,896,256]{2,1,0:T(8,128)(2,1)S(1)} %bitcast.12, bf16[4,2,256,256]{3,2,1,0:T(8,128)(2,1)S(1)} %all_to_all.28.mine_ref, ...), custom_call_target="tpu_custom_call" | custom-call | tf_op jit(solution)/shard_map/final/pallas_call | solution.py:243
  (43 shorter events, 10.0 us)
Async XLA Ops:
  6.5 189.1 %all-gather.5.cloned.1.call-start = ((), (), s32[]{:S(2)}) async-start(), calls=%async_computation.5 | async-start | bytes 7798784 | tf_op jit(solution)/shard_map/all_gather | solution.py:270
  6.5 2.0 copy-start
  8.6 1.2 copy-start.3
  13.8 3.0 %collective-permute-start = (bf16[4,256,256]{2,1,0:T(8,128)(2,1)S(1)}, bf16[4,256,256]{2,1,0:T(8,128)(2,1)S(1)}, u32[]{:S(2)}, u32[]{:S(2)}) collective-permute-start(bf16[4,256,256]{2,1,0:T(8,128)(2,1)S(1)} %get-tuple-element.15), channel_id=1, source_target_pairs={{0,16},{16,0},{1,17},{17,1},{2,18},{18,2},{3,19},{19,3},{4,20},{20... | collective-permute-start | bytes 1572872 | tf_op jit(solution)/shard_map/ppermute | solution.py:204
  41.7 5.5 %collective-permute-start.1 = (bf16[4,256,256]{2,1,0:T(8,128)(2,1)S(1)}, bf16[4,256,256]{2,1,0:T(8,128)(2,1)S(1)}, u32[]{:S(2)}, u32[]{:S(2)}) collective-permute-start(bf16[4,256,256]{2,1,0:T(8,128)(2,1)S(1)} %bitcast.15), channel_id=1, source_target_pairs={{0,16},{16,0},{1,17},{17,1},{2,18},{18,2},{3,19},{19,3},{4,20},{20... | collective-permute-start | bytes 1572872 | tf_op jit(solution)/shard_map/ppermute | solution.py:212
  51.3 2.0 collective-permute-start.2
  75.4 5.8 %collective-permute-start.3 = (bf16[4,256,256]{2,1,0:T(8,128)(2,1)S(1)}, bf16[4,256,256]{2,1,0:T(8,128)(2,1)S(1)}, u32[]{:S(2)}, u32[]{:S(2)}) collective-permute-start(bf16[4,256,256]{2,1,0:T(8,128)(2,1)S(1)} %bitcast.13), channel_id=1, source_target_pairs={{0,16},{16,0},{1,17},{17,1},{2,18},{18,2},{3,19},{19,3},{4,20},{20... | collective-permute-start | bytes 1572872 | tf_op jit(solution)/shard_map/ppermute | solution.py:212
  86.4 2.2 %collective-permute-start.4 = (bf16[4,256,256]{2,1,0:T(8,128)(2,1)S(1)}, bf16[4,256,256]{2,1,0:T(8,128)(2,1)S(1)}, u32[]{:S(2)}, u32[]{:S(2)}) collective-permute-start(bf16[4,256,256]{2,1,0:T(8,128)(2,1)S(1)} %get-tuple-element.20), channel_id=1, source_target_pairs={{0,16},{16,0},{1,17},{17,1},{2,18},{18,2},{3,19},{19,3},{4,20},{20... | collective-permute-start | bytes 1572872 | tf_op jit(solution)/shard_map/ppermute | solution.py:204
  86.9 1.7 collective-permute-start.5
  106.2 2.6 %collective-permute-start.6 = (f32[128,256]{1,0:T(8,128)S(1)}, f32[128,256]{1,0:T(8,128)S(1)}, u32[]{:S(2)}, u32[]{:S(2)}) collective-permute-start(f32[128,256]{1,0:T(8,128)S(1)} %slice_add_fusion.mine_ref), channel_id=1, source_target_pairs={{0,16},{16,0},{1,17},{17,1},{2,18},{18,2},{3,19},{19,3},{4,20},{20... | collective-permute-start | bytes 393224 | tf_op jit(solution)/shard_map/ppermute | solution.py:284
  126.5 6.9 %copy-start.4 = (s32[16]{0:T(128)S(1)}, s32[16]{0:T(128)}, u32[]{:S(2)}) copy-start(s32[16]{0:T(128)} %param.6) | copy-start | bytes 196
  126.5 47.3 %all-to-all-start.3 = ((bf16[16,256,256]{2,1,0:T(8,128)(2,1)}), bf16[16,256,256]{2,1,0:T(8,128)(2,1)S(1)}, u32[]{:S(2)}, u32[]{:S(2)}) async-start(bf16[16,256,256]{2,1,0:T(8,128)(2,1)} %solve.1), calls=%async_computation.3 | async-start | bytes 4194304 | tf_op jit(solution)/shard_map/all_to_all | solution.py:294
  190.9 4.7 %collective-permute-start.7 = (bf16[4,2,256,256]{3,2,1,0:T(8,128)(2,1)S(1)}, bf16[4,2,256,256]{3,2,1,0:T(8,128)(2,1)S(1)}, u32[]{:S(2)}, u32[]{:S(2)}) collective-permute-start(bf16[4,2,256,256]{3,2,1,0:T(8,128)(2,1)S(1)} %all_to_all.28.mine_ref), channel_id=1, source_target_pairs={{0,16},{16,0},{1,17},{17,1},{2,18},{18,2},{3,19},{19,3},{4,20},{20... | collective-permute-start | bytes 3145736 | tf_op jit(solution)/shard_map/ppermute | solution.py:301
  195.6 3.1 %copy-start.1 = (bf16[2,896,2048]{2,1,0:T(8,128)(2,1)S(1)}, bf16[2,896,2048]{2,1,0:T(8,128)(2,1)}, u32[]{:S(2)}) copy-start(bf16[2,896,2048]{2,1,0:T(8,128)(2,1)} %serving_ref.1) | copy-start | bytes 22020100
  198.7 3.1 %copy-start.2 = (bf16[14336,256]{1,0:T(8,128)(2,1)S(1)}, bf16[14336,256]{1,0:T(8,128)(2,1)}, u32[]{:S(2)}) copy-start(bf16[14336,256]{1,0:T(8,128)(2,1)} %all-gather.5.cloned.1.call-done) | copy-start | bytes 22020100
Sparse Core Ops, SparseCore 0:
  86.6 84.5 all-gather.4
where the time goes:
time: 216 us; the launch traced here: 214 us
  blocking collectives  80.6 us (37%)
  waiting for transfers between devices  46.5 us (22%)
  Pallas kernels  36.7 us (17%)
  starting transfers between devices  21.6 us (10%)
  between operations  17.2 us (8%)
  local copies, waits for them, and re-layouts  10.3 us (5%)
    all_to_all x1, waiting for transfers between devices, local(): chunks = lax.all_to_all(solved, EP, 0, 0, tiled=True)  35.7 us
    all_to_all x2, blocking collectives, all_sum(): pieces = lax.all_to_all(chip, 'z', 0, 0, tiled=True)  25 us
    all_gather x2, blocking collectives, all_sum(): step_mine = lax.all_gather(step, 'z', axis=0)  21.6 us
    pallas_call x1, Pallas kernels, solve(): pl.pallas_call(solve_kernel, in_specs=[pl.BlockSpec(memory_space=pltpu.SM...  17.7 us
    all_to_all x1, blocking collectives, local(): pieces = lax.all_to_all(packed, 'z', 0, 0, tiled=True)  17.1 us
    all_to_all x1, blocking collectives, local(): lax.all_to_all(jnp.broadcast_to(picked[None], (4,) + picked.shape), 'z',...  16.9 us
    pallas_call x3, Pallas kernels, sweep(): pl.pallas_call(kernel, in_specs=[SM, ANY] + [VM] * (len(operands) - 2), o...  13.3 us
    unnamed x10, local copies, waits for them, and re-layouts  9.43 us
  transfers between devices with their start and end apart: 10, of which 8 were waited for; matrix products, arithmetic and copies ran while one was open for 1% of the time, Pallas kernels for 8%

commit v1 on v0

v1 whole, which is shorter than its diff:
```python
import jax
import jax.numpy as jnp
from jax import lax
from jax.experimental import pallas as pl
from jax.experimental.pallas import tpu as pltpu
from jax.sharding import Mesh, PartitionSpec as P

D = 7168
FF = 2048
RANK = 256
POWER = 2
SLOTS = 2
N_EP = 16
HALF = RANK // 2
GROUP = 16
CHUNK = FF // 8
SPANS = ((0, 256), (256, 256), (512, 384))
EP = ("x", "y")
SEND, FROM, EXPERT, PRESENT = 0, 8, 10, 12
TILE = 224
SWAP = [(0, 1), (1, 0)]
NT = (((1,), (1,)), ((), ()))
F32 = jnp.float32
BF16 = jnp.bfloat16
VM = pl.BlockSpec(memory_space=pltpu.VMEM)
SM = pl.BlockSpec(memory_space=pltpu.SMEM)
HBM = pl.BlockSpec(memory_space=pltpu.HBM)
TILES = (4, RANK, CHUNK)


def columns(half, j):
    return pl.ds(pl.multiple_of(half * (FF // 2) + j * CHUNK, CHUNK), CHUNK)


def load_rows(a_hbm, a_ref, sems):
    copies = [
        pltpu.make_async_copy(a_hbm.at[pl.ds(s, n)], a_ref.at[pl.ds(s, n)], sems.at[i])
        for i, (s, n) in enumerate(SPANS)
    ]
    for copy in copies:
        copy.start()
    return copies


def power_tiles(c, a_ref, yt_ref, mine_out, other_out):
    for j in range(4):
        tile = jnp.dot(yt_ref[...], a_ref[:, columns(1 - c, j)], preferred_element_type=F32)
        other_out[j] = tile.astype(BF16)
    for j in range(4):
        mine_out[j] = jnp.dot(
            yt_ref[...], a_ref[:, columns(c, j)], preferred_element_type=F32
        )


def sketch_rows(c, a_ref, s, n, mine_ref, other_ref):
    y = None
    for half, steps in ((c, mine_ref), (1 - c, other_ref)):
        for j in range(4):
            term = lax.dot_general(
                a_ref[pl.ds(s, n), columns(half, j)], steps[j], NT, preferred_element_type=F32
            )
            y = term if y is None else y + term
    return y


def first_kernel(
    c_ref, a_hbm, sketch_hbm, mine_out, other_out, a_ref, sketch_ref, yt_ref, sems, sketch_sem
):
    c = c_ref[0]
    sketch_copy = pltpu.make_async_copy(sketch_hbm, sketch_ref, sketch_sem)
    sketch_copy.start()
    copies = load_rows(a_hbm, a_ref, sems)
    sketch_copy.wait()
    for copy, (s, n) in zip(copies, SPANS):
        copy.wait()
        y = jnp.dot(a_ref[pl.ds(s, n), :], sketch_ref[...], preferred_element_type=F32)
        yt_ref[:, pl.ds(s, n)] = y.T.astype(BF16)
    power_tiles(c, a_ref, yt_ref, mine_out, other_out)


def power_kernel(c_ref, a_ref, mine_ref, other_ref, mine_out, other_out, yt_ref):
    c = c_ref[0]
    for s, n in SPANS:
        y = sketch_rows(c, a_ref, s, n, mine_ref, other_ref)
        yt_ref[:, pl.ds(s, n)] = y.T.astype(BF16)
    power_tiles(c, a_ref, yt_ref, mine_out, other_out)


def last_kernel(
    c_ref, a_ref, mine_ref, other_ref,
    y_out, mine_out, other_out, gram_mine, gram_other, yt_ref,
):
    c = c_ref[0]
    for s, n in SPANS:
        y = sketch_rows(c, a_ref, s, n, mine_ref, other_ref)
        y_out[pl.ds(s, n), :] = y.astype(BF16)
        yt_ref[:, pl.ds(s, n)] = y.T.astype(BF16)
    for half, out in ((1 - c, gram_other), (c, gram_mine)):
        turned = yt_ref[pl.ds(pl.multiple_of(half * HALF, HALF), HALF), :]
        out[...] = jnp.dot(turned, y_out[...], preferred_element_type=F32)
    power_tiles(c, a_ref, yt_ref, mine_out, other_out)


def first_pass(c, delta_rows, sketch_matrix):
    rows = delta_rows.shape[0]
    return pl.pallas_call(
        first_kernel,
        in_specs=[SM, HBM, HBM],
        out_specs=[VM] * 2,
        out_shape=[
            jax.ShapeDtypeStruct(TILES, F32),
            jax.ShapeDtypeStruct(TILES, BF16),
        ],
        scratch_shapes=[
            pltpu.VMEM(delta_rows.shape, BF16),
            pltpu.VMEM(sketch_matrix.shape, BF16),
            pltpu.VMEM((RANK, rows), BF16),
            pltpu.SemaphoreType.DMA((len(SPANS),)),
            pltpu.SemaphoreType.DMA,
        ],
        compiler_params=pltpu.CompilerParams(vmem_limit_bytes=16 << 20),
        name="first",
    )(
        c,
        pltpu.with_memory_space_constraint(delta_rows, pltpu.HBM),
        pltpu.with_memory_space_constraint(sketch_matrix, pltpu.HBM),
    )


def power_pass(kernel, c, delta_rows, steps, before, after, name):
    outs = before + [
        jax.ShapeDtypeStruct(TILES, F32), jax.ShapeDtypeStruct(TILES, BF16)
    ] + after
    return pl.pallas_call(
        kernel,
        in_specs=[SM, VM, VM, VM],
        out_specs=[VM] * len(outs),
        out_shape=outs,
        scratch_shapes=[pltpu.VMEM((RANK, delta_rows.shape[0]), BF16)],
        compiler_params=pltpu.CompilerParams(vmem_limit_bytes=24 << 20),
        name=name,
    )(c, delta_rows, *steps)


def exact_dot(a, b):
    return jnp.dot(a, b, preferred_element_type=F32, precision=lax.Precision.HIGHEST)


def invert(a_ref):
    lane = lax.broadcasted_iota(jnp.int32, (GROUP, HALF), 1)
    sub = lax.broadcasted_iota(jnp.int32, (GROUP, HALF), 0)
    lane_all = lax.broadcasted_iota(jnp.int32, (HALF, HALF), 1)

    def spread(row):
        return jnp.broadcast_to(row, (GROUP, HALF))

    def columns_of(rows, base):
        return [jnp.broadcast_to(rows[:, base + i : base + i + 1], (GROUP, HALF)) for i in range(GROUP)]

    def total(terms):
        while len(terms) > 1:
            terms = [terms[i] + terms[i + 1] for i in range(0, len(terms), 2)]
        return terms[0]

    def pivots(base, rows):
        block = columns_of(rows, base)
        for j in range(GROUP):
            inverse = 1.0 / spread(block[j][j : j + 1])
            scaled = block[j] * inverse
            new = []
            for i in range(GROUP):
                if i == j:
                    new.append(jnp.where(sub == j, -inverse, scaled))
                else:
                    t = spread(block[i][j : j + 1])
                    new.append(jnp.where(sub == j, t * inverse, block[i] - scaled * t))
            block = new
        local = lane - base
        rows = jnp.where((local >= 0) & (local < GROUP), jnp.where(local == sub, 1.0, 0.0), -rows)
        return total([block[i] * spread(rows[i : i + 1]) for i in range(GROUP)])

    rows = a_ref[:GROUP, :]
    solved = pivots(0, rows)
    for base in range(0, HALF, GROUP):
        later = base + GROUP
        if later < HALF:
            local = lane - base
            ahead = a_ref[later : later + GROUP, :]
            across = columns_of(ahead, base)
            ahead = jnp.where((local >= 0) & (local < GROUP), 0.0, ahead)
            ahead = ahead - total([across[i] * spread(solved[i : i + 1]) for i in range(GROUP)])
            ahead_solved = pivots(later, ahead)
        here = lane_all - base
        a = jnp.where((here >= 0) & (here < GROUP), 0.0, a_ref[...])
        a_ref[...] = a - lax.dot_general(
            rows, solved, (((0,), (0,)), ((), ())),
            preferred_element_type=F32, precision=lax.Precision.HIGHEST,
        )
        a_ref[base : base + GROUP, :] = solved
        if later < HALF:
            rows, solved = ahead, ahead_solved


def slots_of(owner_ref, owner):
    zero = jnp.int32(0)
    count, expert = zero, [zero] * SLOTS
    for e in range(N_EP):
        hit = owner_ref[e] == owner
        for s in range(SLOTS):
            expert[s] = jnp.where(hit & (count == s), e, expert[s])
        count = count + jnp.where(hit, 1, 0)
    return expert, [jnp.where(count > s, 1, 0) for s in range(SLOTS)]


def write_table(place_ref, owner_ref, table_ref):
    x, y = place_ref[1], place_ref[2]
    for there in range(4):
        expert, _ = slots_of(owner_ref, x * 4 + there)
        for s in range(SLOTS):
            table_ref[SEND + there * SLOTS + s] = expert[s] // 4
    expert, present = slots_of(owner_ref, x * 4 + y)
    for s in range(SLOTS):
        table_ref[FROM + s] = lax.rem(expert[s], 4)
        table_ref[EXPERT + s] = expert[s]
        table_ref[PRESENT + s] = present[s]


def solve_kernel(
    place_ref, owner_ref, mine_ref, other_ref, cross_ref, out_ref, table_ref, a_ref, b_ref, gram_ref
):
    write_table(place_ref, owner_ref, table_ref)
    c = place_ref[0]
    gram_ref[pl.ds(pl.multiple_of(c * HALF, HALF), HALF), :] = mine_ref[...]
    gram_ref[pl.ds(pl.multiple_of((1 - c) * HALF, HALF), HALF), :] = other_ref[...]
    a_ref[...] = gram_ref[:HALF, :HALF]
    invert(a_ref)
    first = -a_ref[...]
    across = gram_ref[:HALF, HALF:]
    step = exact_dot(first, across)
    b_ref[...] = gram_ref[HALF:, HALF:] - exact_dot(across.T, step)
    invert(b_ref)
    top = cross_ref[:HALF]
    low = cross_ref[HALF:]
    low_solved = -exact_dot(b_ref[...], low - exact_dot(step.T, top))
    top_solved = exact_dot(first, top) - exact_dot(step, low_solved)
    top_solved = top_solved.astype(BF16)
    low_solved = low_solved.astype(BF16)
    for x in range(4):
        out_ref[x, :HALF] = top_solved
        out_ref[x, HALF:] = low_solved


def solve(place, owner_of, gram_mine, gram_other, cross):
    return pl.pallas_call(
        solve_kernel,
        in_specs=[SM, SM, VM, VM, VM],
        out_specs=[VM, SM],
        out_shape=[
            jax.ShapeDtypeStruct((4, RANK, cross.shape[1]), BF16),
            jax.ShapeDtypeStruct((16,), jnp.int32),
        ],
        scratch_shapes=[
            pltpu.VMEM((HALF, HALF), F32),
            pltpu.VMEM((HALF, HALF), F32),
            pltpu.VMEM((RANK, RANK), F32),
        ],
        compiler_params=pltpu.CompilerParams(vmem_limit_bytes=12 << 20),
        name="solve",
    )(place, owner_of, gram_mine, gram_other, cross)


def send_kernel(table_ref, tiles_ref, out_ref):
    for there in range(4):
        for s in range(SLOTS):
            out_ref[there, s] = tiles_ref[table_ref[SEND + there * SLOTS + s]]


def keep_kernel(table_ref, tiles_ref, y_hbm, out_ref, y_ref, sems):
    copies = [
        pltpu.make_async_copy(y_hbm.at[table_ref[EXPERT + s]], y_ref.at[s], sems.at[s])
        for s in range(SLOTS)
    ]
    for copy in copies:
        copy.start()
    for s in range(SLOTS):
        tile = tiles_ref[table_ref[FROM + s], s]
        for z in range(4):
            out_ref[z, s] = tile
    for copy in copies:
        copy.wait()


def send(table, tiles):
    return pl.pallas_call(
        send_kernel,
        in_specs=[SM, VM],
        out_specs=VM,
        out_shape=jax.ShapeDtypeStruct((4, SLOTS) + tiles.shape[-2:], BF16),
        compiler_params=pltpu.CompilerParams(vmem_limit_bytes=8 << 20),
        name="send",
    )(table, tiles)


def keep(table, tiles, y_all):
    return pl.pallas_call(
        keep_kernel,
        in_specs=[SM, VM, HBM],
        out_specs=[VM, VM],
        out_shape=[
            jax.ShapeDtypeStruct((4, SLOTS) + tiles.shape[-2:], BF16),
            jax.ShapeDtypeStruct((SLOTS,) + y_all.shape[1:], BF16),
        ],
        scratch_shapes=[pltpu.SemaphoreType.DMA((SLOTS,))],
        compiler_params=pltpu.CompilerParams(vmem_limit_bytes=8 << 20),
        name="keep",
    )(table, tiles, pltpu.with_memory_space_constraint(y_all, pltpu.HBM))


def chip_sum(mine, other):
    return mine + lax.ppermute(other, "c", SWAP).astype(F32)


def all_sum(mine, other):
    chip = chip_sum(mine, other).astype(BF16)
    pieces = lax.all_to_all(chip, "z", 0, 0, tiled=True)
    step = (jnp.sum(pieces.astype(F32), axis=0) / D).astype(BF16)
    step_mine = lax.all_gather(step, "z", axis=0)
    return step_mine, lax.ppermute(step_mine, "c", SWAP)


def final_kernel(
    table_ref, place_ref, y_ref, mine_ref, other_ref, serving_ref, out_hbm, rows_ref, out_sems
):
    c = place_ref[0]
    slots, rows = rows_ref.shape[:2]
    count = rows // TILE

    def span(i):
        return i // count, pl.ds(pl.multiple_of(lax.rem(i, count) * TILE, TILE), TILE)

    def store(i):
        s, here = span(i)
        return pltpu.make_async_copy(rows_ref.at[s, here], out_hbm.at[s, here], out_sems.at[i])

    def step(i, carry):
        s, here = span(i)
        owned = table_ref[PRESENT + s] > 0
        y = y_ref[s, here, :]
        for half, solved in ((c, mine_ref), (1 - c, other_ref)):
            for j in range(4):
                update = jnp.dot(y, solved[j, s], preferred_element_type=F32)
                served = serving_ref[s, here, columns(half, j)].astype(F32)
                summed = served + jnp.where(owned, update, 0.0)
                rows_ref[s, here, columns(half, j)] = summed.astype(BF16)
        store(i).start()
        return carry

    lax.fori_loop(0, slots * count, step, 0)
    for i in range(slots * count):
        store(i).wait()


def final(table, place, y, mine, other, serving):
    slots, rows, _ = serving.shape
    count = slots * (rows // TILE)
    return pl.pallas_call(
        final_kernel,
        in_specs=[SM, SM, VM, VM, VM, VM],
        out_specs=HBM,
        out_shape=jax.ShapeDtypeStruct(serving.shape, BF16),
        scratch_shapes=[
            pltpu.VMEM(serving.shape, BF16),
            pltpu.SemaphoreType.DMA((count,)),
        ],
        compiler_params=pltpu.CompilerParams(vmem_limit_bytes=16 << 20),
        name="final",
    )(table, place, y, mine, other, pltpu.with_memory_space_constraint(serving, pltpu.VMEM))


def local(deltas, sketch_matrix, owner_of, serving):
    c = lax.axis_index("c").astype(jnp.int32).reshape(1)
    place = jnp.stack([lax.axis_index(a) for a in ("c", "x", "y")]).astype(jnp.int32)
    delta_rows = deltas[0]
    rows = delta_rows.shape[0]
    mine, other = first_pass(c, delta_rows, sketch_matrix)
    for iteration in range(POWER - 1):
        steps = all_sum(mine, other)
        mine, other = power_pass(power_kernel, c, delta_rows, steps, [], [], "power")
    steps = all_sum(mine, other)
    sketch, mine, other, gram_mine, gram_other = power_pass(
        last_kernel,
        c,
        delta_rows,
        steps,
        [jax.ShapeDtypeStruct((rows, RANK), BF16)],
        [jax.ShapeDtypeStruct((HALF, RANK), F32)] * 2,
        "last",
    )
    y_all = lax.all_gather(sketch, EP, axis=0)

    gram_chip = chip_sum(gram_mine, gram_other)
    gram_hi = lax.reduce_precision(gram_chip, 8, 7)
    gram_lo = (gram_chip - gram_hi).astype(BF16)
    gram_pair = jnp.concatenate([gram_hi.astype(BF16), gram_lo], axis=0)
    cross_chip = chip_sum(mine, other).astype(BF16)
    packed = jnp.concatenate(
        [cross_chip, jnp.broadcast_to(gram_pair[None], (4, RANK, RANK))], axis=1
    )
    pieces = lax.all_to_all(packed, "z", 0, 0, tiled=True)
    sums = jnp.sum(pieces.astype(F32), axis=0)
    cross = sums[:RANK]
    gram_half = sums[RANK : RANK + HALF] + sums[RANK + HALF :]
    tiles, table = solve(
        place, owner_of, gram_half, lax.ppermute(gram_half, "c", SWAP), cross
    )
    tiles = lax.all_to_all(tiles, "x", 0, 0, tiled=True)
    tiles = lax.all_to_all(send(table, tiles), "y", 0, 0, tiled=True)
    tiles, y = keep(table, tiles, y_all)
    mine = lax.all_to_all(tiles, "z", 0, 0, tiled=True)
    other = lax.ppermute(mine, "c", SWAP)
    return final(table, place, y, mine, other, serving)


def solution(mesh):
    split = Mesh(mesh.devices.reshape(4, 2, 4, 4), ("z", "c", "x", "y"))
    rows = P(EP, ("z", "c"), None)
    return jax.shard_map(
        local,
        mesh=split,
        in_specs=(rows, P(), P(), rows),
        out_specs=rows,
        check_vma=False,
    )
```

time: 216 us -> 197 us (0.912)
  blocking collectives: 80.6 us -> 124 us
  waiting for transfers between devices: 46.5 us -> 10.9 us
  local copies, waits for them, and re-layouts: 10.3 us -> 1.3 us
  starting transfers between devices: 21.6 us -> 14.8 us
  Pallas kernels: 36.7 us -> 30.7 us
  between operations: 17.2 us -> 13.6 us
    all_to_all x1 -> x3, blocking collectives: 16.9 us -> 60.3 us  [the longest x1 23.6 us: local(): tiles = lax.all_to_all(send(table, tiles), 'y', 0, 0, tiled=True)]
    all_to_all x1 -> x0, waiting for transfers between devices: 35.7 us -> none  [local(): chunks = lax.all_to_all(solved, EP, 0, 0, tiled=True)]
    unnamed x10, local copies, waits for them, and re-layouts: 9.43 us -> 1.25 us
    all_to_all x1 -> x0, starting transfers between devices: 6.89 us -> none  [local(): chunks = lax.all_to_all(solved, EP, 0, 0, tiled=True)]
    pallas_call x5 -> x7, Pallas kernels: 36.7 us -> 30.7 us  [the longest x1 10.5 us: solve(): pl.pallas_call(solve_kernel, in_specs=[SM, SM, VM, VM, VM], out_specs=[VM...]
  transfers between devices with their start and end apart: 10 -> 9, of which waited for: 8 -> 7; matrix products, arithmetic and copies ran while one was open for 1% -> 0% of each run, Pallas kernels for 8% -> 5%
where the time goes in v1:
time: 197 us; the launch traced here: 196 us
  blocking collectives  124 us (63%)
  Pallas kernels  30.7 us (16%)
  starting transfers between devices  14.8 us (8%)
  between operations  13.6 us (7%)
  waiting for transfers between devices  10.9 us (6%)
    all_to_all x2, blocking collectives, all_sum(): pieces = lax.all_to_all(chip, 'z', 0, 0, tiled=True)  25 us
    all_to_all x1, blocking collectives, local(): tiles = lax.all_to_all(send(table, tiles), 'y', 0, 0, tiled=True)  23.6 us
    all_gather x2, blocking collectives, all_sum(): step_mine = lax.all_gather(step, 'z', axis=0)  21.6 us
    all_to_all x1, blocking collectives, local(): tiles = lax.all_to_all(tiles, 'x', 0, 0, tiled=True)  19.3 us
    all_to_all x1, blocking collectives, local(): mine = lax.all_to_all(tiles, 'z', 0, 0, tiled=True)  17.4 us
    all_to_all x1, blocking collectives, local(): pieces = lax.all_to_all(packed, 'z', 0, 0, tiled=True)  17.1 us
    pallas_call x1, Pallas kernels, solve(): pl.pallas_call(solve_kernel, in_specs=[SM, SM, VM, VM, VM], out_specs=[VM...  10.5 us
    ppermute x2, starting transfers between devices, all_sum(): return (step_mine, lax.ppermute(step_mine, 'c', SWAP))  8.16 us
  transfers between devices with their start and end apart: 9, of which 7 were waited for; matrix products, arithmetic and copies ran while one was open for 0% of the time, Pallas kernels for 5%

profile of v1, /device:TPU:1, one launch (start us, length us, event | category | flops | bytes accessed | tf_op | source)
XLA Modules:
  0.0 196.2 jit_solution(12478771873692795154)
XLA Ops:
  6.5 5.6 %first.1 = (f32[4,256,256]{2,1,0:T(8,128)S(1)}, bf16[4,256,256]{2,1,0:T(8,128)(2,1)S(1)}) custom-call(s32[1]{0:T(128)} %bitcast.c_ref, bf16[896,2048]{1,0:T(8,128)(2,1)} %bitcast.7, bf16[2048,256]{1,0:T(8,128)(2,1)} %sketch_hbm.1), custom_call_target="tpu_custom_call" | custom-call | tf_op jit(solution)/shard_map/first/pallas_call | solution.py:106
  13.6 1.5 collective-permute-done
  15.3 13.6 %all_to_all.30 = bf16[4,256,256]{2,1,0:T(8,128)(2,1)S(1)} all-to-all(bf16[4,256,256]{2,1,0:T(8,128)(2,1)S(1)} %add_convert_fusion.2), channel_id=1, replica_groups=mesh['z'=4,'c'=2,'x'=4,'y'=4] {'z'}, dimensions={0} | all-to-all | bytes 1048576 | tf_op jit(solution)/shard_map/all_to_all | solution.py:325
  29.0 11.1 %all-gather = bf16[1024,256]{1,0:T(8,128)(2,1)S(1)} all-gather(bf16[256,256]{1,0:T(8,128)(2,1)S(1)} %multiply_convert_fusion.1), channel_id=2, replica_groups=mesh['z'=4,'c'=2,'x'=4,'y'=4] {'z'}, dimensions={0}, use_global_device_ids=true | all-gather | bytes 655360 | tf_op jit(solution)/shard_map/all_gather | solution.py:327
  40.1 3.9 %collective-permute-start.1 = (bf16[4,256,256]{2,1,0:T(8,128)(2,1)S(1)}, bf16[4,256,256]{2,1,0:T(8,128)(2,1)S(1)}, u32[]{:S(2)}, u32[]{:S(2)}) collective-permute-start(bf16[4,256,256]{2,1,0:T(8,128)(2,1)S(1)} %bitcast.14), channel_id=1, source_target_pairs={{0,16},{16,0},{1,17},{17,1},{2,18},{18,2},{3,19},{19,3},{4,20},{20... | collective-permute-start | bytes 1572872 | tf_op jit(solution)/shard_map/ppermute | solution.py:328
  44.0 1.5 collective-permute-done.1.other_ref
  45.5 2.8 %power.1 = (f32[4,256,256]{2,1,0:T(8,128)S(1)}, bf16[4,256,256]{2,1,0:T(8,128)(2,1)S(1)}) custom-call(s32[1]{0:T(128)} %bitcast.c_ref, bf16[896,2048]{1,0:T(8,128)(2,1)S(1)} %bitcast.8, bf16[4,256,256]{2,1,0:T(8,128)(2,1)S(1)} %bitcast.15, bf16[4,256,256]{2,1,0:T(8,128)(2,1)S(1)} %collective-permute-done.1.other_ref), custom_call_target="tpu_custom_call" | custom-call | tf_op jit(solution)/shard_map/power/pallas_call | solution.py:134
  48.8 1.5 collective-permute-done.2
  50.5 11.5 %all_to_all.31 = bf16[4,256,256]{2,1,0:T(8,128)(2,1)S(1)} all-to-all(bf16[4,256,256]{2,1,0:T(8,128)(2,1)S(1)} %add_convert_fusion.1), channel_id=1, replica_groups=mesh['z'=4,'c'=2,'x'=4,'y'=4] {'z'}, dimensions={0} | all-to-all | bytes 1048576 | tf_op jit(solution)/shard_map/all_to_all | solution.py:325
  62.0 10.5 %all-gather.1 = bf16[1024,256]{1,0:T(8,128)(2,1)S(1)} all-gather(bf16[256,256]{1,0:T(8,128)(2,1)S(1)} %multiply_convert_fusion), channel_id=3, replica_groups=mesh['z'=4,'c'=2,'x'=4,'y'=4] {'z'}, dimensions={0}, use_global_device_ids=true | all-gather | bytes 655360 | tf_op jit(solution)/shard_map/all_gather | solution.py:327
  72.5 4.2 %collective-permute-start.3 = (bf16[4,256,256]{2,1,0:T(8,128)(2,1)S(1)}, bf16[4,256,256]{2,1,0:T(8,128)(2,1)S(1)}, u32[]{:S(2)}, u32[]{:S(2)}) collective-permute-start(bf16[4,256,256]{2,1,0:T(8,128)(2,1)S(1)} %bitcast.12), channel_id=1, source_target_pairs={{0,16},{16,0},{1,17},{17,1},{2,18},{18,2},{3,19},{19,3},{4,20},{20... | collective-permute-start | bytes 1572872 | tf_op jit(solution)/shard_map/ppermute | solution.py:328
  76.7 1.5 collective-permute-done.3.other_ref
  78.2 3.9 %last.1 = (bf16[896,256]{1,0:T(8,128)(2,1)}, f32[4,256,256]{2,1,0:T(8,128)S(1)}, bf16[4,256,256]{2,1,0:T(8,128)(2,1)S(1)}, f32[128,256]{1,0:T(8,128)S(1)}, f32[128,256]{1,0:T(8,128)S(1)}) custom-call(s32[1]{0:T(128)} %bitcast.c_ref, bf16[896,2048]{1,0:T(8,128)(2,1)S(1)} %bitcast.9, bf16[4,256,256]{2,1,0:T(8,128)(2,1)S(1)} %bitcast.13, ...), custom_call_target="tpu_custom_call" | custom-call | tf_op jit(solution)/shard_map/last/pallas_call | solution.py:134
  82.8 1.6 collective-permute-done.5
  84.7 17.1 %all_to_all.32 = bf16[4,512,256]{2,1,0:T(8,128)(2,1)S(1)} all-to-all(bf16[4,512,256]{2,1,0:T(8,128)(2,1)S(1)} %pad_maximum_fusion), channel_id=1, replica_groups=mesh['z'=4,'c'=2,'x'=4,'y'=4] {'z'}, dimensions={0} | all-to-all | bytes 2097152 | tf_op jit(solution)/shard_map/all_to_all | solution.py:409
  102.0 1.6 collective-permute-start.6
  104.6 10.5 %solve.1 = (bf16[4,256,256]{2,1,0:T(8,128)(2,1)S(1)}, s32[16]{0:T(128)S(1)}) custom-call(s32[3]{0:T(128)S(1)} %pad_add_fusion.place_ref, s32[16]{0:T(128)S(1)} %copy-done.2, f32[128,256]{1,0:T(8,128)S(1)} %slice_add_fusion.mine_ref, f32[128,256]{1,0:T(8,128)S(1)} %collective-permute-done.6.other_ref, f32[256,256]{1,0:T(8,128)S(1)} %slice.14.cross_ref), custom_call_target="tpu_custom_call" | custom-call | tf_op jit(solution)/shard_map/solve/pallas_call | solution.py:254
  115.1 19.3 %all_to_all.33.tiles_ref = bf16[4,256,256]{2,1,0:T(8,128)(2,1)S(1)} all-to-all(bf16[4,256,256]{2,1,0:T(8,128)(2,1)S(1)} %get-tuple-element.27), channel_id=1, replica_groups=mesh['z'=4,'c'=2,'x'=4,'y'=4] {'x'}, dimensions={0} | all-to-all | bytes 1048576 | tf_op jit(solution)/shard_map/all_to_all | solution.py:416
  135.0 23.6 %all_to_all.34.tiles_ref = bf16[4,2,256,256]{3,2,1,0:T(8,128)(2,1)} all-to-all(bf16[4,2,256,256]{3,2,1,0:T(8,128)(2,1)S(1)} %send.1), channel_id=1, replica_groups=mesh['z'=4,'c'=2,'x'=4,'y'=4] {'y'}, dimensions={0} | all-to-all | bytes 2097152 | tf_op jit(solution)/shard_map/all_to_all | solution.py:417
  159.8 2.0 %keep.1 = (bf16[4,2,256,256]{3,2,1,0:T(8,128)(2,1)S(1)}, bf16[2,896,256]{2,1,0:T(8,128)(2,1)S(1)}) custom-call(s32[16]{0:T(128)S(1)} %get-tuple-element.26.table_ref, bf16[4,2,256,256]{3,2,1,0:T(8,128)(2,1)S(1)} %copy-done.1, bf16[16,896,256]{2,1,0:T(8,128)(2,1)} %bitcast.16), custom_call_target="tpu_custom_call" | custom-call | tf_op jit(solution)/shard_map/keep/pallas_call | solution.py:305
  161.8 17.4 %all_to_all.35.mine_ref = bf16[4,2,256,256]{3,2,1,0:T(8,128)(2,1)S(1)} all-to-all(bf16[4,2,256,256]{3,2,1,0:T(8,128)(2,1)S(1)} %get-tuple-element.30), channel_id=1, replica_groups=mesh['z'=4,'c'=2,'x'=4,'y'=4] {'z'}, dimensions={0} | all-to-all | bytes 2097152 | tf_op jit(solution)/shard_map/all_to_all | solution.py:419
  179.2 2.5 %collective-permute-start.7 = (bf16[4,2,256,256]{3,2,1,0:T(8,128)(2,1)S(1)}, bf16[4,2,256,256]{3,2,1,0:T(8,128)(2,1)S(1)}, u32[]{:S(2)}, u32[]{:S(2)}) collective-permute-start(bf16[4,2,256,256]{3,2,1,0:T(8,128)(2,1)S(1)} %all_to_all.35.mine_ref), channel_id=1, source_target_pairs={{0,16},{16,0},{1,17},{17,1},{2,18},{18,2},{3,19},{19,3},{4,20},{20... | collective-permute-start | bytes 3145736 | tf_op jit(solution)/shard_map/ppermute | solution.py:420
  181.7 2.3 %collective-permute-done.7.other_ref = bf16[4,2,256,256]{3,2,1,0:T(8,128)(2,1)S(1)} collective-permute-done((bf16[4,2,256,256]{3,2,1,0:T(8,128)(2,1)S(1)}, bf16[4,2,256,256]{3,2,1,0:T(8,128)(2,1)S(1)}, u32[]{:S(2)}, u32[]{:S(2)}) %collective-permute-start.7) | collective-permute-done | bytes 1048608 | tf_op jit(solution)/shard_map/ppermute | solution.py:420
  184.0 5.3 %final.1 = bf16[2,896,2048]{2,1,0:T(8,128)(2,1)} custom-call(s32[16]{0:T(128)S(1)} %get-tuple-element.26.table_ref, s32[3]{0:T(128)S(1)} %pad_add_fusion.place_ref, bf16[2,896,256]{2,1,0:T(8,128)(2,1)S(1)} %get-tuple-element.29.y_ref, bf16[4,2,256,256]{3,2,1,0:T(8,128)(2,1)S(1)} %all_to_all.35.mine_ref, ...), custom_call_target="tpu_custom_call" | custom-call | tf_op jit(solution)/shard_map/final/pallas_call | solution.py:366
  (36 shorter events, 6.2 us)
Async XLA Ops:
  6.5 152.0 %all-gather.5.cloned.1.call-start = ((), (), s32[]{:S(2)}) async-start(), calls=%async_computation.6 | async-start | bytes 7798784 | tf_op jit(solution)/shard_map/all_gather | solution.py:399
  12.1 33.4 %copy-start = (bf16[1,896,2048]{2,1,0:T(8,128)(2,1)S(1)}, bf16[1,896,2048]{2,1,0:T(8,128)(2,1)}, u32[]{:S(2)}) copy-start(bf16[1,896,2048]{2,1,0:T(8,128)(2,1)} %param.4) | copy-start | bytes 11010052
  12.2 3.0 %collective-permute-start = (bf16[4,256,256]{2,1,0:T(8,128)(2,1)S(1)}, bf16[4,256,256]{2,1,0:T(8,128)(2,1)S(1)}, u32[]{:S(2)}, u32[]{:S(2)}) collective-permute-start(bf16[4,256,256]{2,1,0:T(8,128)(2,1)S(1)} %get-tuple-element.19), channel_id=1, source_target_pairs={{0,16},{16,0},{1,17},{17,1},{2,18},{18,2},{3,19},{19,3},{4,20},{20... | collective-permute-start | bytes 1572872 | tf_op jit(solution)/shard_map/ppermute | solution.py:320
  40.1 5.5 %collective-permute-start.1 = (bf16[4,256,256]{2,1,0:T(8,128)(2,1)S(1)}, bf16[4,256,256]{2,1,0:T(8,128)(2,1)S(1)}, u32[]{:S(2)}, u32[]{:S(2)}) collective-permute-start(bf16[4,256,256]{2,1,0:T(8,128)(2,1)S(1)} %bitcast.14), channel_id=1, source_target_pairs={{0,16},{16,0},{1,17},{17,1},{2,18},{18,2},{3,19},{19,3},{4,20},{20... | collective-permute-start | bytes 1572872 | tf_op jit(solution)/shard_map/ppermute | solution.py:328
  48.3 2.0 %collective-permute-start.2 = (bf16[4,256,256]{2,1,0:T(8,128)(2,1)S(1)}, bf16[4,256,256]{2,1,0:T(8,128)(2,1)S(1)}, u32[]{:S(2)}, u32[]{:S(2)}) collective-permute-start(bf16[4,256,256]{2,1,0:T(8,128)(2,1)S(1)} %get-tuple-element.21), channel_id=1, source_target_pairs={{0,16},{16,0},{1,17},{17,1},{2,18},{18,2},{3,19},{19,3},{4,20},{20... | collective-permute-start | bytes 1572872 | tf_op jit(solution)/shard_map/ppermute | solution.py:320
  72.5 5.8 %collective-permute-start.3 = (bf16[4,256,256]{2,1,0:T(8,128)(2,1)S(1)}, bf16[4,256,256]{2,1,0:T(8,128)(2,1)S(1)}, u32[]{:S(2)}, u32[]{:S(2)}) collective-permute-start(bf16[4,256,256]{2,1,0:T(8,128)(2,1)S(1)} %bitcast.12), channel_id=1, source_target_pairs={{0,16},{16,0},{1,17},{17,1},{2,18},{18,2},{3,19},{19,3},{4,20},{20... | collective-permute-start | bytes 1572872 | tf_op jit(solution)/shard_map/ppermute | solution.py:328
  82.2 2.2 %collective-permute-start.4 = (bf16[4,256,256]{2,1,0:T(8,128)(2,1)S(1)}, bf16[4,256,256]{2,1,0:T(8,128)(2,1)S(1)}, u32[]{:S(2)}, u32[]{:S(2)}) collective-permute-start(bf16[4,256,256]{2,1,0:T(8,128)(2,1)S(1)} %get-tuple-element.23), channel_id=1, source_target_pairs={{0,16},{16,0},{1,17},{17,1},{2,18},{18,2},{3,19},{19,3},{4,20},{20... | collective-permute-start | bytes 1572872 | tf_op jit(solution)/shard_map/ppermute | solution.py:320
  82.6 1.7 collective-permute-start.5
  84.5 20.0 %copy-start.2 = (s32[16]{0:T(128)S(1)}, s32[16]{0:T(128)}, u32[]{:S(2)}) copy-start(s32[16]{0:T(128)} %owner_ref.1) | copy-start | bytes 196
  102.0 2.6 %collective-permute-start.6 = (f32[128,256]{1,0:T(8,128)S(1)}, f32[128,256]{1,0:T(8,128)S(1)}, u32[]{:S(2)}, u32[]{:S(2)}) collective-permute-start(f32[128,256]{1,0:T(8,128)S(1)} %slice_add_fusion.mine_ref), channel_id=1, source_target_pairs={{0,16},{16,0},{1,17},{17,1},{2,18},{18,2},{3,19},{19,3},{4,20},{20... | collective-permute-start | bytes 393224 | tf_op jit(solution)/shard_map/ppermute | solution.py:414
  134.3 49.7 %slice-start = ((s8[7340032]{0:T(1024)(128)(4,1)}), s8[3145728]{0:T(1024)(128)(4,1)S(1)}, s32[]{:S(2)}) async-start(s8[7340032]{0:T(1024)(128)(4,1)} %bitcast.10), calls=%async_computation.7 | async-start | bytes 6291456
  158.6 1.2 copy-start.1
  159.8 24.2 %slice-start.1 = ((s8[7340032]{0:T(1024)(128)(4,1)}), s8[4194304]{0:T(1024)(128)(4,1)S(1)}, s32[]{:S(2)}) async-start(s8[7340032]{0:T(1024)(128)(4,1)} %bitcast.10), calls=%async_computation.8 | async-start | bytes 8388608
  179.2 4.8 %collective-permute-start.7 = (bf16[4,2,256,256]{3,2,1,0:T(8,128)(2,1)S(1)}, bf16[4,2,256,256]{3,2,1,0:T(8,128)(2,1)S(1)}, u32[]{:S(2)}, u32[]{:S(2)}) collective-permute-start(bf16[4,2,256,256]{3,2,1,0:T(8,128)(2,1)S(1)} %all_to_all.35.mine_ref), channel_id=1, source_target_pairs={{0,16},{16,0},{1,17},{17,1},{2,18},{18,2},{3,19},{19,3},{4,20},{20... | collective-permute-start | bytes 3145736 | tf_op jit(solution)/shard_map/ppermute | solution.py:420
Sparse Core Ops, SparseCore 0:
  82.3 70.8 all-gather.4

commit v2 on v1

--- a/solution.py
+++ b/solution.py
@@ -1,9 +1,12 @@
+import functools
+
 import jax
 import jax.numpy as jnp
 from jax import lax
 from jax.experimental import pallas as pl
 from jax.experimental.pallas import tpu as pltpu
 from jax.sharding import Mesh, PartitionSpec as P
+
 
 D = 7168
 FF = 2048
@@ -13,11 +16,13 @@
 N_EP = 16
 HALF = RANK // 2
 GROUP = 16
+EXTRA = 16
 CHUNK = FF // 8
 SPANS = ((0, 256), (256, 256), (512, 384))
 EP = ("x", "y")
 SEND, FROM, EXPERT, PRESENT = 0, 8, 10, 12
-TILE = 224
+TILE = 448
+STEPS = (0, 3, 1, 2)
 SWAP = [(0, 1), (1, 0)]
 NT = (((1,), (1,)), ((), ()))
 F32 = jnp.float32
@@ -95,9 +100,17 @@
         y = sketch_rows(c, a_ref, s, n, mine_ref, other_ref)
         y_out[pl.ds(s, n), :] = y.astype(BF16)
         yt_ref[:, pl.ds(s, n)] = y.T.astype(BF16)
-    for half, out in ((1 - c, gram_other), (c, gram_mine)):
-        turned = yt_ref[pl.ds(pl.multiple_of(half * HALF, HALF), HALF), :]
-        out[...] = jnp.dot(turned, y_out[...], preferred_element_type=F32)
+    gram = jnp.dot(yt_ref[...], y_out[...], preferred_element_type=F32)
+    top, low = gram[:HALF, :HALF], gram[HALF:, HALF:]
+    row = lax.broadcasted_iota(jnp.int32, (HALF, HALF), 0)
+    col = lax.broadcasted_iota(jnp.int32, (HALF, HALF), 1)
+    diagonal = jnp.sum(jnp.where(row == col, top, 0.0), axis=0, keepdims=True)
+    square = jnp.where(row > col, top, low)
+    gram_mine[:HALF] = jnp.where(c == 0, square, gram[:HALF, HALF:])
+    gram_other[:HALF] = jnp.where(c == 0, gram[:HALF, HALF:], square)
+    below = jnp.broadcast_to(diagonal, (EXTRA, HALF))
+    gram_mine[HALF:] = jnp.where(c == 0, below, 0.0)
+    gram_other[HALF:] = jnp.where(c == 0, 0.0, below)
     power_tiles(c, a_ref, yt_ref, mine_out, other_out)
 
 
@@ -127,7 +140,7 @@
     )
 
 
-def power_pass(kernel, c, delta_rows, steps, before, after, name):
+def power_pass(kernel, c, delta_rows, steps, before, after):
     outs = before + [
         jax.ShapeDtypeStruct(TILES, F32), jax.ShapeDtypeStruct(TILES, BF16)
     ] + after
@@ -138,7 +151,6 @@
         out_shape=outs,
         scratch_shapes=[pltpu.VMEM((RANK, delta_rows.shape[0]), BF16)],
         compiler_params=pltpu.CompilerParams(vmem_limit_bytes=24 << 20),
-        name=name,
     )(c, delta_rows, *steps)
 
 
@@ -226,18 +238,24 @@
 
 
 def solve_kernel(
-    place_ref, owner_ref, mine_ref, other_ref, cross_ref, out_ref, table_ref, a_ref, b_ref, gram_ref
+    place_ref, owner_ref, mine_ref, other_ref, cross_ref, out_ref, table_ref, a_ref, b_ref
 ):
     write_table(place_ref, owner_ref, table_ref)
     c = place_ref[0]
-    gram_ref[pl.ds(pl.multiple_of(c * HALF, HALF), HALF), :] = mine_ref[...]
-    gram_ref[pl.ds(pl.multiple_of((1 - c) * HALF, HALF), HALF), :] = other_ref[...]
-    a_ref[...] = gram_ref[:HALF, :HALF]
+    square = jnp.where(c == 0, mine_ref[...], other_ref[...])
+    across = jnp.where(c == 0, other_ref[:HALF], mine_ref[:HALF])
+    diagonal = square[HALF : HALF + 1]
+    square = square[:HALF]
+    row = lax.broadcasted_iota(jnp.int32, (HALF, HALF), 0)
+    col = lax.broadcasted_iota(jnp.int32, (HALF, HALF), 1)
+    lower = jnp.where(row > col, square, 0.0)
+    upper = jnp.where(row < col, square, 0.0)
+    a_ref[...] = lower + lower.T + jnp.where(row == col, diagonal, 0.0)
+    b_ref[...] = upper + upper.T + jnp.where(row == col, square, 0.0)
     invert(a_ref)
     first = -a_ref[...]
-    across = gram_ref[:HALF, HALF:]
     step = exact_dot(first, across)
-    b_ref[...] = gram_ref[HALF:, HALF:] - exact_dot(across.T, step)
+    b_ref[...] = b_ref[...] - exact_dot(across.T, step)
     invert(b_ref)
     top = cross_ref[:HALF]
     low = cross_ref[HALF:]
@@ -262,7 +280,6 @@
         scratch_shapes=[
             pltpu.VMEM((HALF, HALF), F32),
             pltpu.VMEM((HALF, HALF), F32),
-            pltpu.VMEM((RANK, RANK), F32),
         ],
         compiler_params=pltpu.CompilerParams(vmem_limit_bytes=12 << 20),
         name="solve",
@@ -275,17 +292,15 @@
             out_ref[there, s] = tiles_ref[table_ref[SEND + there * SLOTS + s]]
 
 
-def keep_kernel(table_ref, tiles_ref, y_hbm, out_ref, y_ref, sems):
-    copies = [
-        pltpu.make_async_copy(y_hbm.at[table_ref[EXPERT + s]], y_ref.at[s], sems.at[s])
-        for s in range(SLOTS)
-    ]
+def keep_kernel(table_ref, tiles_hbm, y_hbm, out_ref, y_ref, sems):
+    copies = []
+    for s in range(SLOTS):
+        tile = tiles_hbm.at[table_ref[FROM + s], s]
+        copies.append(pltpu.make_async_copy(tile, out_ref.at[s], sems.at[s, 0]))
+        sketch = y_hbm.at[table_ref[EXPERT + s]]
+        copies.append(pltpu.make_async_copy(sketch, y_ref.at[s], sems.at[s, 1]))
     for copy in copies:
         copy.start()
-    for s in range(SLOTS):
-        tile = tiles_ref[table_ref[FROM + s], s]
-        for z in range(4):
-            out_ref[z, s] = tile
     for copy in copies:
         copy.wait()
 
@@ -304,16 +319,20 @@
 def keep(table, tiles, y_all):
     return pl.pallas_call(
         keep_kernel,
-        in_specs=[SM, VM, HBM],
+        in_specs=[SM, HBM, HBM],
         out_specs=[VM, VM],
         out_shape=[
-            jax.ShapeDtypeStruct((4, SLOTS) + tiles.shape[-2:], BF16),
+            jax.ShapeDtypeStruct(tiles.shape[1:], BF16),
             jax.ShapeDtypeStruct((SLOTS,) + y_all.shape[1:], BF16),
         ],
-        scratch_shapes=[pltpu.SemaphoreType.DMA((SLOTS,))],
+        scratch_shapes=[pltpu.SemaphoreType.DMA((SLOTS, 2))],
         compiler_params=pltpu.CompilerParams(vmem_limit_bytes=8 << 20),
         name="keep",
-    )(table, tiles, pltpu.with_memory_space_constraint(y_all, pltpu.HBM))
+    )(
+        table,
+        pltpu.with_memory_space_constraint(tiles, pltpu.HBM),
+        pltpu.with_memory_space_constraint(y_all, pltpu.HBM),
+    )
 
 
 def chip_sum(mine, other):
@@ -324,68 +343,87 @@
     chip = chip_sum(mine, other).astype(BF16)
     pieces = lax.all_to_all(chip, "z", 0, 0, tiled=True)
     step = (jnp.sum(pieces.astype(F32), axis=0) / D).astype(BF16)
-    step_mine = lax.all_gather(step, "z", axis=0)
+    step_mine = lax.all_to_all(
+        jnp.broadcast_to(step[None], (4,) + step.shape), "z", 0, 0, tiled=True
+    )
     return step_mine, lax.ppermute(step_mine, "c", SWAP)
 
 
 def final_kernel(
-    table_ref, place_ref, y_ref, mine_ref, other_ref, serving_ref, out_hbm, rows_ref, out_sems
+    step, table_ref, place_ref, y_ref, mine_ref, other_ref, serving_ref, begun_hbm, out_hbm, rows_ref, sems
 ):
+    del begun_hbm
     c = place_ref[0]
-    slots, rows = rows_ref.shape[:2]
+    there = lax.rem(place_ref[3] + step, 4)
+    slots, rows = rows_ref.shape[1:3]
     count = rows // TILE
 
     def span(i):
         return i // count, pl.ds(pl.multiple_of(lax.rem(i, count) * TILE, TILE), TILE)
 
-    def store(i):
+    def store(i, side):
         s, here = span(i)
-        return pltpu.make_async_copy(rows_ref.at[s, here], out_hbm.at[s, here], out_sems.at[i])
-
-    def step(i, carry):
+        half = c if side == 0 else 1 - c
+        return pltpu.make_async_copy(
+            rows_ref.at[side, s, here],
+            out_hbm.at[s, here, columns(half, there)],
+            sems.at[side, i],
+        )
+
+    def update(i, carry):
         s, here = span(i)
         owned = table_ref[PRESENT + s] > 0
         y = y_ref[s, here, :]
-        for half, solved in ((c, mine_ref), (1 - c, other_ref)):
-            for j in range(4):
-                update = jnp.dot(y, solved[j, s], preferred_element_type=F32)
-                served = serving_ref[s, here, columns(half, j)].astype(F32)
-                summed = served + jnp.where(owned, update, 0.0)
-                rows_ref[s, here, columns(half, j)] = summed.astype(BF16)
-        store(i).start()
+        for side, tiles in enumerate((mine_ref, other_ref)):
+            half = c if side == 0 else 1 - c
+            term = jnp.dot(y, tiles[s], preferred_element_type=F32)
+            served = serving_ref[s, here, columns(half, there)].astype(F32)
+            summed = served + jnp.where(owned, term, 0.0)
+            rows_ref[side, s, here, :] = summed.astype(BF16)
+            store(i, side).start()
         return carry
 
-    lax.fori_loop(0, slots * count, step, 0)
+    lax.fori_loop(0, slots * count, update, 0)
     for i in range(slots * count):
-        store(i).wait()
-
-
-def final(table, place, y, mine, other, serving):
+        for side in range(2):
+            store(i, side).wait()
+
+
+def final_first_kernel(step, table_ref, place_ref, y_ref, mine_ref, other_ref, serving_ref, *refs):
+    final_kernel(step, table_ref, place_ref, y_ref, mine_ref, other_ref, serving_ref, None, *refs)
+
+
+def final(step, table, place, y, mine, other, serving, begun):
     slots, rows, _ = serving.shape
-    count = slots * (rows // TILE)
-    return pl.pallas_call(
-        final_kernel,
-        in_specs=[SM, SM, VM, VM, VM, VM],
+    more = [] if begun is None else [begun]
+    kernel = final_first_kernel if begun is None else final_kernel
+    return pl.pallas_call(
+        functools.partial(kernel, step),
+        in_specs=[SM, SM, VM, VM, VM, VM] + [HBM] * len(more),
         out_specs=HBM,
         out_shape=jax.ShapeDtypeStruct(serving.shape, BF16),
+        input_output_aliases={6: 0} if more else {},
         scratch_shapes=[
-            pltpu.VMEM(serving.shape, BF16),
-            pltpu.SemaphoreType.DMA((count,)),
-        ],
-        compiler_params=pltpu.CompilerParams(vmem_limit_bytes=16 << 20),
+            pltpu.VMEM((2, slots, rows, CHUNK), BF16),
+            pltpu.SemaphoreType.DMA((2, slots * (rows // TILE))),
+        ],
+        compiler_params=pltpu.CompilerParams(vmem_limit_bytes=6 << 20),
+        cost_estimate=pl.CostEstimate(
+            flops=serving.size * RANK // 2, bytes_accessed=serving.size, transcendentals=0
+        ),
         name="final",
-    )(table, place, y, mine, other, pltpu.with_memory_space_constraint(serving, pltpu.VMEM))
+    )(table, place, y, mine, other, serving, *more)
 
 
 def local(deltas, sketch_matrix, owner_of, serving):
     c = lax.axis_index("c").astype(jnp.int32).reshape(1)
-    place = jnp.stack([lax.axis_index(a) for a in ("c", "x", "y")]).astype(jnp.int32)
+    place = jnp.stack([lax.axis_index(a) for a in ("c", "x", "y", "z")]).astype(jnp.int32)
     delta_rows = deltas[0]
     rows = delta_rows.shape[0]
     mine, other = first_pass(c, delta_rows, sketch_matrix)
-    for iteration in range(POWER - 1):
+    for _ in range(POWER - 1):
         steps = all_sum(mine, other)
-        mine, other = power_pass(power_kernel, c, delta_rows, steps, [], [], "power")
+        mine, other = power_pass(power_kernel, c, delta_rows, steps, [], [])
     steps = all_sum(mine, other)
     sketch, mine, other, gram_mine, gram_other = power_pass(
         last_kernel,
@@ -393,32 +431,37 @@
         delta_rows,
         steps,
         [jax.ShapeDtypeStruct((rows, RANK), BF16)],
-        [jax.ShapeDtypeStruct((HALF, RANK), F32)] * 2,
-        "last",
+        [jax.ShapeDtypeStruct((HALF + EXTRA, HALF), F32)] * 2,
     )
     y_all = lax.all_gather(sketch, EP, axis=0)
 
     gram_chip = chip_sum(gram_mine, gram_other)
     gram_hi = lax.reduce_precision(gram_chip, 8, 7)
     gram_lo = (gram_chip - gram_hi).astype(BF16)
-    gram_pair = jnp.concatenate([gram_hi.astype(BF16), gram_lo], axis=0)
+    gram_pair = jnp.concatenate([gram_hi.astype(BF16), gram_lo], axis=1)
     cross_chip = chip_sum(mine, other).astype(BF16)
     packed = jnp.concatenate(
-        [cross_chip, jnp.broadcast_to(gram_pair[None], (4, RANK, RANK))], axis=1
+        [cross_chip, jnp.broadcast_to(gram_pair[None], (4,) + gram_pair.shape)], axis=1
     )
     pieces = lax.all_to_all(packed, "z", 0, 0, tiled=True)
     sums = jnp.sum(pieces.astype(F32), axis=0)
     cross = sums[:RANK]
-    gram_half = sums[RANK : RANK + HALF] + sums[RANK + HALF :]
+    gram_half = sums[RANK:, :HALF] + sums[RANK:, HALF:]
     tiles, table = solve(
         place, owner_of, gram_half, lax.ppermute(gram_half, "c", SWAP), cross
     )
     tiles = lax.all_to_all(tiles, "x", 0, 0, tiled=True)
     tiles = lax.all_to_all(send(table, tiles), "y", 0, 0, tiled=True)
-    tiles, y = keep(table, tiles, y_all)
-    mine = lax.all_to_all(tiles, "z", 0, 0, tiled=True)
-    other = lax.ppermute(mine, "c", SWAP)
-    return final(table, place, y, mine, other, serving)
+    tile, y = keep(table, tiles, y_all)
+    serving = pltpu.with_memory_space_constraint(serving, pltpu.VMEM)
+    moved = {0: tile}
+    updated = None
+    for step in STEPS[1:]:
+        moved[step] = lax.ppermute(tile, "z", [((z + step) % 4, z) for z in range(4)])
+    for step in STEPS:
+        other = lax.ppermute(moved[step], "c", SWAP)
+        updated = final(step, table, place, y, moved[step], other, serving, updated)
+    return updated
 
 
 def solution(mesh):

time: 197 us -> 191 us (0.970)
  blocking collectives: 124 us -> 89.3 us
  starting transfers between devices: 14.8 us -> 27.4 us
  waiting for transfers between devices: 10.9 us -> 22.5 us
  Pallas kernels: 30.7 us -> 35.9 us
    all_gather x2 -> x0, blocking collectives: 21.6 us -> none  [all_sum(): step_mine = lax.all_gather(step, 'z', axis=0)]
    all_to_all x2, blocking collectives: 34.5 us -> 20.9 us  [all_sum(): lax.all_to_all(jnp.broadcast_to(step[None], (4,) + step.shape), 'z', 0, 0...]
    ppermute x1 -> x7, starting transfers between devices: 2.54 us -> 15.1 us  [the longest x4 10.8 us: local(): other = lax.ppermute(moved[step], 'c', SWAP)]
    all_to_all x0 -> x1, waiting for transfers between devices: none -> 12.3 us  [local(): pieces = lax.all_to_all(packed, 'z', 0, 0, tiled=True)]
    pallas_call x2 -> x5, Pallas kernels: 7.28 us -> 12.5 us  [the longest x4 10.4 us: final(): pl.pallas_call(functools.partial(kernel, step), in_specs=[SM, SM, VM, VM,...]
    all_to_all x0 -> x1, starting transfers between devices: none -> 3.5 us  [local(): pieces = lax.all_to_all(packed, 'z', 0, 0, tiled=True)]
    ppermute x2, starting transfers between devices: 8.16 us -> 4.74 us  [all_sum(): return (step_mine, lax.ppermute(step_mine, 'c', SWAP))]
  transfers between devices with their start and end apart: 9 -> 16, of which waited for: 7 -> 8; matrix products, arithmetic and copies ran while one was open for 0% -> 1% of each run, Pallas kernels for 5% -> 10%
where the time goes in v2:
time: 191 us
  blocking collectives  89.3 us (47%)
  Pallas kernels  35.9 us (19%)
  starting transfers between devices  27.4 us (14%)
  waiting for transfers between devices  22.5 us (12%)
  between operations  13.6 us (7%)
    all_to_all x2, blocking collectives, all_sum(): pieces = lax.all_to_all(chip, 'z', 0, 0, tiled=True)  25.2 us
    all_to_all x1, blocking collectives, local(): tiles = lax.all_to_all(send(table, tiles), 'y', 0, 0, tiled=True)  24 us
    all_to_all x2, blocking collectives, all_sum(): lax.all_to_all(jnp.broadcast_to(step[None], (4,) + step.shape), 'z', 0, 0...  20.9 us
    all_to_all x1, blocking collectives, local(): tiles = lax.all_to_all(tiles, 'x', 0, 0, tiled=True)  19.3 us
    all_to_all x1, waiting for transfers between devices, local(): pieces = lax.all_to_all(packed, 'z', 0, 0, tiled=True)  12.3 us
    ppermute x4, starting transfers between devices, local(): other = lax.ppermute(moved[step], 'c', SWAP)  10.8 us
    pallas_call x1, Pallas kernels, solve(): pl.pallas_call(solve_kernel, in_specs=[SM, SM, VM, VM, VM], out_specs=[VM...  10.5 us
    pallas_call x4, Pallas kernels, final(): pl.pallas_call(functools.partial(kernel, step), in_specs=[SM, SM, VM, VM,...  10.4 us
  transfers between devices with their start and end apart: 16, of which 8 were waited for; matrix products, arithmetic and copies ran while one was open for 1% of the time, Pallas kernels for 10%

profile of v2, /device:TPU:1, one launch (start us, length us, event | category | flops | bytes accessed | tf_op | source)
XLA Modules:
  0.0 190.6 jit_solution(4757073596884697065)
XLA Ops:
  6.5 5.8 %first.1 = (f32[4,256,256]{2,1,0:T(8,128)S(1)}, bf16[4,256,256]{2,1,0:T(8,128)(2,1)S(1)}) custom-call(s32[1]{0:T(128)} %bitcast.c_ref, bf16[896,2048]{1,0:T(8,128)(2,1)} %bitcast.8, bf16[2048,256]{1,0:T(8,128)(2,1)} %sketch_hbm.1), custom_call_target="tpu_custom_call" | custom-call | tf_op jit(solution)/shard_map/first/pallas_call | solution.py:119
  15.4 13.6 %all_to_all.35 = bf16[4,256,256]{2,1,0:T(8,128)(2,1)S(1)} all-to-all(bf16[4,256,256]{2,1,0:T(8,128)(2,1)S(1)} %add_convert_fusion.2), channel_id=1, replica_groups=mesh['z'=4,'c'=2,'x'=4,'y'=4] {'z'}, dimensions={0} | all-to-all | bytes 1048576 | tf_op jit(solution)/shard_map/all_to_all | solution.py:344
  29.2 10.2 %all_to_all.36.mine_ref = bf16[4,256,256]{2,1,0:T(8,128)(2,1)S(1)} all-to-all(bf16[4,256,256]{2,1,0:T(8,128)(2,1)S(1)} %broadcast_in_dim.6), channel_id=1, replica_groups=mesh['z'=4,'c'=2,'x'=4,'y'=4] {'z'}, dimensions={0} | all-to-all | bytes 1048576 | tf_op jit(solution)/shard_map/all_to_all | solution.py:346
  39.3 2.7 %collective-permute-start.1 = (bf16[4,256,256]{2,1,0:T(8,128)(2,1)S(1)}, bf16[4,256,256]{2,1,0:T(8,128)(2,1)S(1)}, u32[]{:S(2)}, u32[]{:S(2)}) collective-permute-start(bf16[4,256,256]{2,1,0:T(8,128)(2,1)S(1)} %all_to_all.36.mine_ref), channel_id=1, source_target_pairs={{0,16},{16,0},{1,17},{17,1},{2,18},{18,2},{3,19},{19,3},{4,20},{20... | collective-permute-start | bytes 1572872 | tf_op jit(solution)/shard_map/ppermute | solution.py:349
  43.5 2.8 %shard_map.46 = (f32[4,256,256]{2,1,0:T(8,128)S(1)}, bf16[4,256,256]{2,1,0:T(8,128)(2,1)S(1)}) custom-call(s32[1]{0:T(128)} %bitcast.c_ref, bf16[896,2048]{1,0:T(8,128)(2,1)S(1)} %bitcast.9, bf16[4,256,256]{2,1,0:T(8,128)(2,1)S(1)} %all_to_all.36.mine_ref, bf16[4,256,256]{2,1,0:T(8,128)(2,1)S(1)} %collective-permute-done.1.other_ref), custom_call_target="tpu_custom_call" | custom-call | tf_op jit(solution)/shard_map/pallas_call | solution.py:147
  48.4 11.6 %all_to_all.37 = bf16[4,256,256]{2,1,0:T(8,128)(2,1)S(1)} all-to-all(bf16[4,256,256]{2,1,0:T(8,128)(2,1)S(1)} %add_convert_fusion.1), channel_id=1, replica_groups=mesh['z'=4,'c'=2,'x'=4,'y'=4] {'z'}, dimensions={0} | all-to-all | bytes 1048576 | tf_op jit(solution)/shard_map/all_to_all | solution.py:344
  60.2 10.7 %all_to_all.38.mine_ref = bf16[4,256,256]{2,1,0:T(8,128)(2,1)S(1)} all-to-all(bf16[4,256,256]{2,1,0:T(8,128)(2,1)S(1)} %broadcast_in_dim.7), channel_id=1, replica_groups=mesh['z'=4,'c'=2,'x'=4,'y'=4] {'z'}, dimensions={0} | all-to-all | bytes 1048576 | tf_op jit(solution)/shard_map/all_to_all | solution.py:346
  70.9 2.1 %collective-permute-start.3 = (bf16[4,256,256]{2,1,0:T(8,128)(2,1)S(1)}, bf16[4,256,256]{2,1,0:T(8,128)(2,1)S(1)}, u32[]{:S(2)}, u32[]{:S(2)}) collective-permute-start(bf16[4,256,256]{2,1,0:T(8,128)(2,1)S(1)} %all_to_all.38.mine_ref), channel_id=1, source_target_pairs={{0,16},{16,0},{1,17},{17,1},{2,18},{18,2},{3,19},{19,3},{4,20},{20... | collective-permute-start | bytes 1572872 | tf_op jit(solution)/shard_map/ppermute | solution.py:349
  74.6 3.8 %shard_map.47 = (bf16[896,256]{1,0:T(8,128)(2,1)}, f32[4,256,256]{2,1,0:T(8,128)S(1)}, bf16[4,256,256]{2,1,0:T(8,128)(2,1)S(1)}, f32[144,128]{1,0:T(8,128)S(1)}, f32[144,128]{1,0:T(8,128)S(1)}) custom-call(s32[1]{0:T(128)} %bitcast.c_ref, bf16[896,2048]{1,0:T(8,128)(2,1)S(1)} %bitcast.10, bf16[4,256,256]{2,1,0:T(8,128)(2,1)S(1)} %all_to_all.38.mine_ref, ...), custom_call_target="tpu_custom_call" | custom-call | tf_op jit(solution)/shard_map/pallas_call | solution.py:147
  81.6 3.5 %all-to-all-start.4 = ((bf16[4,400,256]{2,1,0:T(8,128)(2,1)}), bf16[4,400,256]{2,1,0:T(8,128)(2,1)S(1)}, u32[]{:S(2)}, u32[]{:S(2)}) async-start(bf16[4,400,256]{2,1,0:T(8,128)(2,1)} %pad_maximum_fusion), calls=%async_computation.4 | async-start | bytes 1638400 | tf_op jit(solution)/shard_map/all_to_all | solution.py:446
  85.1 12.3 %all-to-all-done.4 = bf16[4,400,256]{2,1,0:T(8,128)(2,1)S(1)} async-done(((bf16[4,400,256]{2,1,0:T(8,128)(2,1)}), bf16[4,400,256]{2,1,0:T(8,128)(2,1)S(1)}, u32[]{:S(2)}, u32[]{:S(2)}) %all-to-all-start.4) | async-done | bytes 819232 | tf_op jit(solution)/shard_map/all_to_all | solution.py:446
  100.0 10.5 %solve.1 = (bf16[4,256,256]{2,1,0:T(8,128)(2,1)S(1)}, s32[16]{0:T(128)S(1)}) custom-call(s32[4]{0:T(128)S(1)} %pad_add_fusion.place_ref, s32[16]{0:T(128)S(1)} %copy-done.1, f32[144,128]{1,0:T(8,128)S(1)} %slice_add_fusion.mine_ref, f32[144,128]{1,0:T(8,128)S(1)} %collective-permute-done.6.other_ref, f32[256,256]{1,0:T(8,128)S(1)} %slice.14.cross_ref), custom_call_target="tpu_custom_call" | custom-call | tf_op jit(solution)/shard_map/solve/pallas_call | solution.py:272
  110.5 19.3 %all_to_all.39.tiles_ref = bf16[4,256,256]{2,1,0:T(8,128)(2,1)S(1)} all-to-all(bf16[4,256,256]{2,1,0:T(8,128)(2,1)S(1)} %get-tuple-element.27), channel_id=1, replica_groups=mesh['z'=4,'c'=2,'x'=4,'y'=4] {'x'}, dimensions={0} | all-to-all | bytes 1048576 | tf_op jit(solution)/shard_map/all_to_all | solution.py:453
  130.4 24.0 %all_to_all.40.tiles_hbm = bf16[4,2,256,256]{3,2,1,0:T(8,128)(2,1)} all-to-all(bf16[4,2,256,256]{3,2,1,0:T(8,128)(2,1)S(1)} %send.1), channel_id=1, replica_groups=mesh['z'=4,'c'=2,'x'=4,'y'=4] {'y'}, dimensions={0} | all-to-all | bytes 2097152 | tf_op jit(solution)/shard_map/all_to_all | solution.py:454
  154.4 2.1 %keep.1 = (bf16[2,256,256]{2,1,0:T(8,128)(2,1)S(1)}, bf16[2,896,256]{2,1,0:T(8,128)(2,1)S(1)}) custom-call(s32[16]{0:T(128)S(1)} %get-tuple-element.26.table_ref, bf16[4,2,256,256]{3,2,1,0:T(8,128)(2,1)} %all_to_all.40.tiles_hbm, bf16[16,896,256]{2,1,0:T(8,128)(2,1)} %bitcast.11), custom_call_target="tpu_custom_call" | custom-call | tf_op jit(solution)/shard_map/keep/pallas_call | solution.py:320
  160.9 2.0 %collective-permute-start.13 = (bf16[2,256,256]{2,1,0:T(8,128)(2,1)S(1)}, bf16[2,256,256]{2,1,0:T(8,128)(2,1)S(1)}, u32[]{:S(2)}, u32[]{:S(2)}) collective-permute-start(bf16[2,256,256]{2,1,0:T(8,128)(2,1)S(1)} %get-tuple-element.30.mine_ref), channel_id=1, source_target_pairs={{0,16},{16,0},{1,17},{17,1},{2,18},{18,2},{3,19},{19,3},{4,20},{20... | collective-permute-start | bytes 786440 | tf_op jit(solution)/shard_map/ppermute | solution.py:462
  162.9 1.7 collective-permute-done.11.mine_ref
  164.5 2.4 %collective-permute-start.12 = (bf16[2,256,256]{2,1,0:T(8,128)(2,1)S(1)}, bf16[2,256,256]{2,1,0:T(8,128)(2,1)S(1)}, u32[]{:S(2)}, u32[]{:S(2)}) collective-permute-start(bf16[2,256,256]{2,1,0:T(8,128)(2,1)S(1)} %collective-permute-done.11.mine_ref), channel_id=1, source_target_pairs={{0,16},{16,0},{1,17},{17,1},{2,18},{18,2},{3,19},{19,3},{4,20},{20... | collective-permute-start | bytes 786440 | tf_op jit(solution)/shard_map/ppermute | solution.py:462
  166.9 4.6 %collective-permute-start.10 = (bf16[2,256,256]{2,1,0:T(8,128)(2,1)S(1)}, bf16[2,256,256]{2,1,0:T(8,128)(2,1)S(1)}, u32[]{:S(2)}, u32[]{:S(2)}) collective-permute-start(bf16[2,256,256]{2,1,0:T(8,128)(2,1)S(1)} %collective-permute-done.9.mine_ref), channel_id=1, source_target_pairs={{0,16},{16,0},{1,17},{17,1},{2,18},{18,2},{3,19},{19,3},{4,20},{20... | collective-permute-start | bytes 786440 | tf_op jit(solution)/shard_map/ppermute | solution.py:462
  171.5 1.8 collective-permute-start.8
  173.3 2.6 %final.4.begun_hbm = bf16[2,896,2048]{2,1,0:T(8,128)(2,1)} custom-call(s32[16]{0:T(128)S(1)} %get-tuple-element.26.table_ref, s32[4]{0:T(128)S(1)} %pad_add_fusion.place_ref, bf16[2,896,256]{2,1,0:T(8,128)(2,1)S(1)} %get-tuple-element.29.y_ref, bf16[2,256,256]{2,1,0:T(8,128)(2,1)S(1)} %get-tuple-element.30.mine_ref, ...), custom_call_target="tpu_custom_call" | custom-call | flops 469762048 | bytes 3670016 | tf_op jit(solution)/shard_map/final/pallas_call | solution.py:400
  176.0 2.6 %final.5.begun_hbm = bf16[2,896,2048]{2,1,0:T(8,128)(2,1)} custom-call(s32[16]{0:T(128)S(1)} %get-tuple-element.26.table_ref, s32[4]{0:T(128)S(1)} %pad_add_fusion.place_ref, bf16[2,896,256]{2,1,0:T(8,128)(2,1)S(1)} %get-tuple-element.29.y_ref, bf16[2,256,256]{2,1,0:T(8,128)(2,1)S(1)} %collective-permute-done.11.mine_ref, ...), custom_call_target="tpu_custom_call", output_to_operand_aliasing={{}: (6, {})} | custom-call | flops 469762048 | bytes 3670016 | tf_op jit(solution)/shard_map/final/pallas_call | solution.py:400
  178.6 2.6 %final.6.begun_hbm = bf16[2,896,2048]{2,1,0:T(8,128)(2,1)} custom-call(s32[16]{0:T(128)S(1)} %get-tuple-element.26.table_ref, s32[4]{0:T(128)S(1)} %pad_add_fusion.place_ref, bf16[2,896,256]{2,1,0:T(8,128)(2,1)S(1)} %get-tuple-element.29.y_ref, bf16[2,256,256]{2,1,0:T(8,128)(2,1)S(1)} %collective-permute-done.9.mine_ref, ...), custom_call_target="tpu_custom_call", output_to_operand_aliasing={{}: (6, {})} | custom-call | flops 469762048 | bytes 3670016 | tf_op jit(solution)/shard_map/final/pallas_call | solution.py:400
  181.2 2.6 %final.7 = bf16[2,896,2048]{2,1,0:T(8,128)(2,1)} custom-call(s32[16]{0:T(128)S(1)} %get-tuple-element.26.table_ref, s32[4]{0:T(128)S(1)} %pad_add_fusion.place_ref, bf16[2,896,256]{2,1,0:T(8,128)(2,1)S(1)} %get-tuple-element.29.y_ref, bf16[2,256,256]{2,1,0:T(8,128)(2,1)S(1)} %collective-permute-done.7.mine_ref, ...), custom_call_target="tpu_custom_call", output_to_operand_aliasing={{}: (6, {})} | custom-call | flops 469762048 | bytes 3670016 | tf_op jit(solution)/shard_map/final/pallas_call | solution.py:400
  (51 shorter events, 19.4 us)
Async XLA Ops:
  6.5 147.8 %all-gather.3.cloned.1.call-start = ((), (), s32[]{:S(2)}) async-start(), calls=%async_computation.7 | async-start | bytes 7798784 | tf_op jit(solution)/shard_map/all_gather | solution.py:436
  6.5 37.0 %copy-start = (bf16[1,896,2048]{2,1,0:T(8,128)(2,1)S(1)}, bf16[1,896,2048]{2,1,0:T(8,128)(2,1)}, u32[]{:S(2)}) copy-start(bf16[1,896,2048]{2,1,0:T(8,128)(2,1)} %param.4) | copy-start | bytes 11010052
  12.3 3.0 %collective-permute-start = (bf16[4,256,256]{2,1,0:T(8,128)(2,1)S(1)}, bf16[4,256,256]{2,1,0:T(8,128)(2,1)S(1)}, u32[]{:S(2)}, u32[]{:S(2)}) collective-permute-start(bf16[4,256,256]{2,1,0:T(8,128)(2,1)S(1)} %get-tuple-element.19), channel_id=1, source_target_pairs={{0,16},{16,0},{1,17},{17,1},{2,18},{18,2},{3,19},{19,3},{4,20},{20... | collective-permute-start | bytes 1572872 | tf_op jit(solution)/shard_map/ppermute | solution.py:339
  39.3 4.2 %collective-permute-start.1 = (bf16[4,256,256]{2,1,0:T(8,128)(2,1)S(1)}, bf16[4,256,256]{2,1,0:T(8,128)(2,1)S(1)}, u32[]{:S(2)}, u32[]{:S(2)}) collective-permute-start(bf16[4,256,256]{2,1,0:T(8,128)(2,1)S(1)} %all_to_all.36.mine_ref), channel_id=1, source_target_pairs={{0,16},{16,0},{1,17},{17,1},{2,18},{18,2},{3,19},{19,3},{4,20},{20... | collective-permute-start | bytes 1572872 | tf_op jit(solution)/shard_map/ppermute | solution.py:349
  46.3 2.0 %collective-permute-start.2 = (bf16[4,256,256]{2,1,0:T(8,128)(2,1)S(1)}, bf16[4,256,256]{2,1,0:T(8,128)(2,1)S(1)}, u32[]{:S(2)}, u32[]{:S(2)}) collective-permute-start(bf16[4,256,256]{2,1,0:T(8,128)(2,1)S(1)} %get-tuple-element.21), channel_id=1, source_target_pairs={{0,16},{16,0},{1,17},{17,1},{2,18},{18,2},{3,19},{19,3},{4,20},{20... | collective-permute-start | bytes 1572872 | tf_op jit(solution)/shard_map/ppermute | solution.py:339
  60.2 39.8 %copy-start.1 = (s32[16]{0:T(128)S(1)}, s32[16]{0:T(128)}, u32[]{:S(2)}) copy-start(s32[16]{0:T(128)} %owner_ref.1) | copy-start | bytes 196
  70.9 3.6 %collective-permute-start.3 = (bf16[4,256,256]{2,1,0:T(8,128)(2,1)S(1)}, bf16[4,256,256]{2,1,0:T(8,128)(2,1)S(1)}, u32[]{:S(2)}, u32[]{:S(2)}) collective-permute-start(bf16[4,256,256]{2,1,0:T(8,128)(2,1)S(1)} %all_to_all.38.mine_ref), channel_id=1, source_target_pairs={{0,16},{16,0},{1,17},{17,1},{2,18},{18,2},{3,19},{19,3},{4,20},{20... | collective-permute-start | bytes 1572872 | tf_op jit(solution)/shard_map/ppermute | solution.py:349
  78.4 2.1 %collective-permute-start.4 = (bf16[4,256,256]{2,1,0:T(8,128)(2,1)S(1)}, bf16[4,256,256]{2,1,0:T(8,128)(2,1)S(1)}, u32[]{:S(2)}, u32[]{:S(2)}) collective-permute-start(bf16[4,256,256]{2,1,0:T(8,128)(2,1)S(1)} %get-tuple-element.23), channel_id=1, source_target_pairs={{0,16},{16,0},{1,17},{17,1},{2,18},{18,2},{3,19},{19,3},{4,20},{20... | collective-permute-start | bytes 1572872 | tf_op jit(solution)/shard_map/ppermute | solution.py:339
  78.8 1.6 collective-permute-start.5
  81.6 15.8 %all-to-all-start.4 = ((bf16[4,400,256]{2,1,0:T(8,128)(2,1)}), bf16[4,400,256]{2,1,0:T(8,128)(2,1)S(1)}, u32[]{:S(2)}, u32[]{:S(2)}) async-start(bf16[4,400,256]{2,1,0:T(8,128)(2,1)} %pad_maximum_fusion), calls=%async_computation.4 | async-start | bytes 1638400 | tf_op jit(solution)/shard_map/all_to_all | solution.py:446
  97.6 75.7 %slice-start = ((s8[7340032]{0:T(1024)(128)(4,1)}), s8[3145728]{0:T(1024)(128)(4,1)S(1)}, s32[]{:S(2)}) async-start(s8[7340032]{0:T(1024)(128)(4,1)} %bitcast.6), calls=%async_computation.8 | async-start | bytes 6291456
  97.6 2.4 %collective-permute-start.6 = (f32[144,128]{1,0:T(8,128)S(1)}, f32[144,128]{1,0:T(8,128)S(1)}, u32[]{:S(2)}, u32[]{:S(2)}) collective-permute-start(f32[144,128]{1,0:T(8,128)S(1)} %slice_add_fusion.mine_ref), channel_id=1, source_target_pairs={{0,16},{16,0},{1,17},{17,1},{2,18},{18,2},{3,19},{19,3},{4,20},{20... | collective-permute-start | bytes 221192 | tf_op jit(solution)/shard_map/ppermute | solution.py:451
  154.4 18.9 %slice-start.1 = ((s8[7340032]{0:T(1024)(128)(4,1)}), s8[4194304]{0:T(1024)(128)(4,1)S(1)}, s32[]{:S(2)}) async-start(s8[7340032]{0:T(1024)(128)(4,1)} %bitcast.6), calls=%async_computation.9 | async-start | bytes 8388608
  156.5 8.0 %collective-permute-start.11 = (bf16[2,256,256]{2,1,0:T(8,128)(2,1)S(1)}, bf16[2,256,256]{2,1,0:T(8,128)(2,1)S(1)}, u32[]{:S(2)}, u32[]{:S(2)}) collective-permute-start(bf16[2,256,256]{2,1,0:T(8,128)(2,1)S(1)} %get-tuple-element.30.mine_ref), channel_id=1, source_target_pairs={{96,0},{0,32},{32,64},{64,96},{97,1},{1,33},{33,65},{65,97},{98,2}... | collective-permute-start | bytes 786440 | tf_op jit(solution)/shard_map/ppermute | solution.py:460
  157.8 9.1 %collective-permute-start.9 = (bf16[2,256,256]{2,1,0:T(8,128)(2,1)S(1)}, bf16[2,256,256]{2,1,0:T(8,128)(2,1)S(1)}, u32[]{:S(2)}, u32[]{:S(2)}) collective-permute-start(bf16[2,256,256]{2,1,0:T(8,128)(2,1)S(1)} %get-tuple-element.30.mine_ref), channel_id=1, source_target_pairs={{32,0},{64,32},{96,64},{0,96},{33,1},{65,33},{97,65},{1,97},{34,2}... | collective-permute-start | bytes 786440 | tf_op jit(solution)/shard_map/ppermute | solution.py:460
  159.3 12.2 %collective-permute-start.7 = (bf16[2,256,256]{2,1,0:T(8,128)(2,1)S(1)}, bf16[2,256,256]{2,1,0:T(8,128)(2,1)S(1)}, u32[]{:S(2)}, u32[]{:S(2)}) collective-permute-start(bf16[2,256,256]{2,1,0:T(8,128)(2,1)S(1)} %get-tuple-element.30.mine_ref), channel_id=1, source_target_pairs={{64,0},{96,32},{0,64},{32,96},{65,1},{97,33},{1,65},{33,97},{66,2}... | collective-permute-start | bytes 786440 | tf_op jit(solution)/shard_map/ppermute | solution.py:460
  160.9 12.4 %collective-permute-start.13 = (bf16[2,256,256]{2,1,0:T(8,128)(2,1)S(1)}, bf16[2,256,256]{2,1,0:T(8,128)(2,1)S(1)}, u32[]{:S(2)}, u32[]{:S(2)}) collective-permute-start(bf16[2,256,256]{2,1,0:T(8,128)(2,1)S(1)} %get-tuple-element.30.mine_ref), channel_id=1, source_target_pairs={{0,16},{16,0},{1,17},{17,1},{2,18},{18,2},{3,19},{19,3},{4,20},{20... | collective-permute-start | bytes 786440 | tf_op jit(solution)/shard_map/ppermute | solution.py:462
  164.5 11.4 %collective-permute-start.12 = (bf16[2,256,256]{2,1,0:T(8,128)(2,1)S(1)}, bf16[2,256,256]{2,1,0:T(8,128)(2,1)S(1)}, u32[]{:S(2)}, u32[]{:S(2)}) collective-permute-start(bf16[2,256,256]{2,1,0:T(8,128)(2,1)S(1)} %collective-permute-done.11.mine_ref), channel_id=1, source_target_pairs={{0,16},{16,0},{1,17},{17,1},{2,18},{18,2},{3,19},{19,3},{4,20},{20... | collective-permute-start | bytes 786440 | tf_op jit(solution)/shard_map/ppermute | solution.py:462
  166.9 11.7 %collective-permute-start.10 = (bf16[2,256,256]{2,1,0:T(8,128)(2,1)S(1)}, bf16[2,256,256]{2,1,0:T(8,128)(2,1)S(1)}, u32[]{:S(2)}, u32[]{:S(2)}) collective-permute-start(bf16[2,256,256]{2,1,0:T(8,128)(2,1)S(1)} %collective-permute-done.9.mine_ref), channel_id=1, source_target_pairs={{0,16},{16,0},{1,17},{17,1},{2,18},{18,2},{3,19},{19,3},{4,20},{20... | collective-permute-start | bytes 786440 | tf_op jit(solution)/shard_map/ppermute | solution.py:462
  171.5 9.7 %collective-permute-start.8 = (bf16[2,256,256]{2,1,0:T(8,128)(2,1)S(1)}, bf16[2,256,256]{2,1,0:T(8,128)(2,1)S(1)}, u32[]{:S(2)}, u32[]{:S(2)}) collective-permute-start(bf16[2,256,256]{2,1,0:T(8,128)(2,1)S(1)} %collective-permute-done.7.mine_ref), channel_id=1, source_target_pairs={{0,16},{16,0},{1,17},{17,1},{2,18},{18,2},{3,19},{19,3},{4,20},{20... | collective-permute-start | bytes 786440 | tf_op jit(solution)/shard_map/ppermute | solution.py:462
Sparse Core Ops, SparseCore 0:
  78.5 71.1 all-gather.2

commit v3 on v2

--- a/solution.py
+++ b/solution.py
@@ -23,6 +23,14 @@
 SEND, FROM, EXPERT, PRESENT = 0, 8, 10, 12
 TILE = 448
 STEPS = (0, 3, 1, 2)
+STAGES = (
+    ((0, False), (0, True)),
+    ((3, False),),
+    ((3, True),),
+    ((1, False),),
+    ((1, True), (2, False)),
+    ((2, True),),
+)
 SWAP = [(0, 1), (1, 0)]
 NT = (((1,), (1,)), ((), ()))
 F32 = jnp.float32
@@ -69,9 +77,9 @@
 
 
 def first_kernel(
-    c_ref, a_hbm, sketch_hbm, mine_out, other_out, a_ref, sketch_ref, yt_ref, sems, sketch_sem
+    a_hbm, sketch_hbm, mine_out, other_out, a_ref, sketch_ref, yt_ref, sems, sketch_sem
 ):
-    c = c_ref[0]
+    c = lax.axis_index("c")
     sketch_copy = pltpu.make_async_copy(sketch_hbm, sketch_ref, sketch_sem)
     sketch_copy.start()
     copies = load_rows(a_hbm, a_ref, sems)
@@ -83,8 +91,8 @@
     power_tiles(c, a_ref, yt_ref, mine_out, other_out)
 
 
-def power_kernel(c_ref, a_ref, mine_ref, other_ref, mine_out, other_out, yt_ref):
-    c = c_ref[0]
+def power_kernel(a_ref, mine_ref, other_ref, mine_out, other_out, yt_ref):
+    c = lax.axis_index("c")
     for s, n in SPANS:
         y = sketch_rows(c, a_ref, s, n, mine_ref, other_ref)
         yt_ref[:, pl.ds(s, n)] = y.T.astype(BF16)
@@ -92,10 +100,10 @@
 
 
 def last_kernel(
-    c_ref, a_ref, mine_ref, other_ref,
+    a_ref, mine_ref, other_ref,
     y_out, mine_out, other_out, gram_mine, gram_other, yt_ref,
 ):
-    c = c_ref[0]
+    c = lax.axis_index("c")
     for s, n in SPANS:
         y = sketch_rows(c, a_ref, s, n, mine_ref, other_ref)
         y_out[pl.ds(s, n), :] = y.astype(BF16)
@@ -114,11 +122,11 @@
     power_tiles(c, a_ref, yt_ref, mine_out, other_out)
 
 
-def first_pass(c, delta_rows, sketch_matrix):
+def first_pass(delta_rows, sketch_matrix):
     rows = delta_rows.shape[0]
     return pl.pallas_call(
         first_kernel,
-        in_specs=[SM, HBM, HBM],
+        in_specs=[HBM, HBM],
         out_specs=[VM] * 2,
         out_shape=[
             jax.ShapeDtypeStruct(TILES, F32),
@@ -134,24 +142,23 @@
         compiler_params=pltpu.CompilerParams(vmem_limit_bytes=16 << 20),
         name="first",
     )(
-        c,
         pltpu.with_memory_space_constraint(delta_rows, pltpu.HBM),
         pltpu.with_memory_space_constraint(sketch_matrix, pltpu.HBM),
     )
 
 
-def power_pass(kernel, c, delta_rows, steps, before, after):
+def power_pass(kernel, delta_rows, steps, before, after):
     outs = before + [
         jax.ShapeDtypeStruct(TILES, F32), jax.ShapeDtypeStruct(TILES, BF16)
     ] + after
     return pl.pallas_call(
         kernel,
-        in_specs=[SM, VM, VM, VM],
+        in_specs=[VM, VM, VM],
         out_specs=[VM] * len(outs),
         out_shape=outs,
         scratch_shapes=[pltpu.VMEM((RANK, delta_rows.shape[0]), BF16)],
         compiler_params=pltpu.CompilerParams(vmem_limit_bytes=24 << 20),
-    )(c, delta_rows, *steps)
+    )(delta_rows, *steps)
 
 
 def exact_dot(a, b):
@@ -224,8 +231,8 @@
     return expert, [jnp.where(count > s, 1, 0) for s in range(SLOTS)]
 
 
-def write_table(place_ref, owner_ref, table_ref):
-    x, y = place_ref[1], place_ref[2]
+def write_table(owner_ref, table_ref):
+    x, y = lax.axis_index("x"), lax.axis_index("y")
     for there in range(4):
         expert, _ = slots_of(owner_ref, x * 4 + there)
         for s in range(SLOTS):
@@ -238,10 +245,10 @@
 
 
 def solve_kernel(
-    place_ref, owner_ref, mine_ref, other_ref, cross_ref, out_ref, table_ref, a_ref, b_ref
+    owner_ref, mine_ref, other_ref, cross_ref, out_ref, table_ref, a_ref, b_ref
 ):
-    write_table(place_ref, owner_ref, table_ref)
-    c = place_ref[0]
+    write_table(owner_ref, table_ref)
+    c = lax.axis_index("c")
     square = jnp.where(c == 0, mine_ref[...], other_ref[...])
     across = jnp.where(c == 0, other_ref[:HALF], mine_ref[:HALF])
     diagonal = square[HALF : HALF + 1]
@@ -263,18 +270,17 @@
     top_solved = exact_dot(first, top) - exact_dot(step, low_solved)
     top_solved = top_solved.astype(BF16)
     low_solved = low_solved.astype(BF16)
-    for x in range(4):
-        out_ref[x, :HALF] = top_solved
-        out_ref[x, HALF:] = low_solved
-
-
-def solve(place, owner_of, gram_mine, gram_other, cross):
+    out_ref[:HALF] = top_solved
+    out_ref[HALF:] = low_solved
+
+
+def solve(owner_of, gram_mine, gram_other, cross):
     return pl.pallas_call(
         solve_kernel,
-        in_specs=[SM, SM, VM, VM, VM],
+        in_specs=[SM, VM, VM, VM],
         out_specs=[VM, SM],
         out_shape=[
-            jax.ShapeDtypeStruct((4, RANK, cross.shape[1]), BF16),
+            jax.ShapeDtypeStruct((RANK, cross.shape[1]), BF16),
             jax.ShapeDtypeStruct((16,), jnp.int32),
         ],
         scratch_shapes=[
@@ -283,46 +289,76 @@
         ],
         compiler_params=pltpu.CompilerParams(vmem_limit_bytes=12 << 20),
         name="solve",
-    )(place, owner_of, gram_mine, gram_other, cross)
-
-
-def send_kernel(table_ref, tiles_ref, out_ref):
-    for there in range(4):
+    )(owner_of, gram_mine, gram_other, cross)
+
+
+def send_kernel(table_ref, *refs):
+    tiles_refs, out_refs, all_ref = refs[:4], refs[4:8], refs[8]
+    for step, tile_ref in enumerate(tiles_refs):
+        all_ref[lax.rem(lax.axis_index("x") - step + 4, 4)] = tile_ref[...]
+    for step, out_ref in enumerate(out_refs):
+        there = lax.rem(lax.axis_index("y") + step, 4)
         for s in range(SLOTS):
-            out_ref[there, s] = tiles_ref[table_ref[SEND + there * SLOTS + s]]
-
-
-def keep_kernel(table_ref, tiles_hbm, y_hbm, out_ref, y_ref, sems):
-    copies = []
+            out_ref[s] = all_ref[table_ref[SEND + there * SLOTS + s]]
+
+
+def keep_kernel(table_ref, *refs):
+    *tiles_hbm, y_hbm, out_ref, y_ref, sems = refs
+
+    def tile_copy(s, tiles):
+        return pltpu.make_async_copy(tiles.at[s], out_ref.at[s], sems.at[s, 0])
+
+    def sketch_copy(s):
+        sketch = y_hbm.at[table_ref[EXPERT + s]]
+        return pltpu.make_async_copy(sketch, y_ref.at[s], sems.at[s, 1])
+
     for s in range(SLOTS):
-        tile = tiles_hbm.at[table_ref[FROM + s], s]
-        copies.append(pltpu.make_async_copy(tile, out_ref.at[s], sems.at[s, 0]))
-        sketch = y_hbm.at[table_ref[EXPERT + s]]
-        copies.append(pltpu.make_async_copy(sketch, y_ref.at[s], sems.at[s, 1]))
-    for copy in copies:
-        copy.start()
-    for copy in copies:
-        copy.wait()
+        present = table_ref[PRESENT + s] > 0
+        steps = lax.rem(lax.axis_index("y") - table_ref[FROM + s] + 4, 4)
+
+        @pl.when(present)
+        def _():
+            sketch_copy(s).start()
+
+        for step, tiles in enumerate(tiles_hbm):
+
+            @pl.when(present & (steps == step))
+            def _():
+                tile_copy(s, tiles).start()
+
+        @pl.when(table_ref[PRESENT + s] == 0)
+        def _():
+            out_ref[s] = jnp.zeros_like(out_ref[s])
+            y_ref[s] = jnp.zeros_like(y_ref[s])
+
+    for s in range(SLOTS):
+
+        @pl.when(table_ref[PRESENT + s] > 0)
+        def _():
+            tile_copy(s, tiles_hbm[0]).wait()
+            sketch_copy(s).wait()
 
 
 def send(table, tiles):
+    shape = tiles[0].shape
     return pl.pallas_call(
         send_kernel,
-        in_specs=[SM, VM],
-        out_specs=VM,
-        out_shape=jax.ShapeDtypeStruct((4, SLOTS) + tiles.shape[-2:], BF16),
+        in_specs=[SM] + [VM] * 4,
+        out_specs=[VM] * 4,
+        out_shape=[jax.ShapeDtypeStruct((SLOTS,) + shape, BF16)] * 4,
+        scratch_shapes=[pltpu.VMEM((4,) + shape, BF16)],
         compiler_params=pltpu.CompilerParams(vmem_limit_bytes=8 << 20),
         name="send",
-    )(table, tiles)
+    )(table, *tiles)
 
 
 def keep(table, tiles, y_all):
     return pl.pallas_call(
         keep_kernel,
-        in_specs=[SM, HBM, HBM],
+        in_specs=[SM] + [HBM] * 5,
         out_specs=[VM, VM],
         out_shape=[
-            jax.ShapeDtypeStruct(tiles.shape[1:], BF16),
+            jax.ShapeDtypeStruct(tiles[0].shape, BF16),
             jax.ShapeDtypeStruct((SLOTS,) + y_all.shape[1:], BF16),
         ],
         scratch_shapes=[pltpu.SemaphoreType.DMA((SLOTS, 2))],
@@ -330,7 +366,7 @@
         name="keep",
     )(
         table,
-        pltpu.with_memory_space_constraint(tiles, pltpu.HBM),
+        *(pltpu.with_memory_space_constraint(t, pltpu.HBM) for t in tiles),
         pltpu.with_memory_space_constraint(y_all, pltpu.HBM),
     )
 
@@ -349,85 +385,75 @@
     return step_mine, lax.ppermute(step_mine, "c", SWAP)
 
 
-def final_kernel(
-    step, table_ref, place_ref, y_ref, mine_ref, other_ref, serving_ref, begun_hbm, out_hbm, rows_ref, sems
-):
-    del begun_hbm
-    c = place_ref[0]
-    there = lax.rem(place_ref[3] + step, 4)
+def final_kernel(parts, y_ref, serving_ref, *refs):
+    tiles_refs, (out_hbm, rows_ref, sems) = refs[: len(parts)], refs[-3:]
+    c = lax.axis_index("c")
     slots, rows = rows_ref.shape[1:3]
     count = rows // TILE
 
     def span(i):
         return i // count, pl.ds(pl.multiple_of(lax.rem(i, count) * TILE, TILE), TILE)
 
-    def store(i, side):
+    def side(p):
+        step, shared = parts[p]
+        there = lax.rem(lax.axis_index("z") + step, 4)
+        return columns(1 - c if shared else c, there)
+
+    def store(i, p):
         s, here = span(i)
-        half = c if side == 0 else 1 - c
         return pltpu.make_async_copy(
-            rows_ref.at[side, s, here],
-            out_hbm.at[s, here, columns(half, there)],
-            sems.at[side, i],
+            rows_ref.at[p, s, here], out_hbm.at[s, here, side(p)], sems.at[p, i]
         )
 
     def update(i, carry):
         s, here = span(i)
-        owned = table_ref[PRESENT + s] > 0
         y = y_ref[s, here, :]
-        for side, tiles in enumerate((mine_ref, other_ref)):
-            half = c if side == 0 else 1 - c
+        for p, tiles in enumerate(tiles_refs):
             term = jnp.dot(y, tiles[s], preferred_element_type=F32)
-            served = serving_ref[s, here, columns(half, there)].astype(F32)
-            summed = served + jnp.where(owned, term, 0.0)
-            rows_ref[side, s, here, :] = summed.astype(BF16)
-            store(i, side).start()
+            served = serving_ref[s, here, side(p)].astype(F32)
+            rows_ref[p, s, here, :] = (served + term).astype(BF16)
+            store(i, p).start()
         return carry
 
     lax.fori_loop(0, slots * count, update, 0)
     for i in range(slots * count):
-        for side in range(2):
-            store(i, side).wait()
-
-
-def final_first_kernel(step, table_ref, place_ref, y_ref, mine_ref, other_ref, serving_ref, *refs):
-    final_kernel(step, table_ref, place_ref, y_ref, mine_ref, other_ref, serving_ref, None, *refs)
-
-
-def final(step, table, place, y, mine, other, serving, begun):
+        for p in range(len(parts)):
+            store(i, p).wait()
+
+
+def final(parts, tiles, y, serving, begun):
     slots, rows, _ = serving.shape
     more = [] if begun is None else [begun]
-    kernel = final_first_kernel if begun is None else final_kernel
     return pl.pallas_call(
-        functools.partial(kernel, step),
-        in_specs=[SM, SM, VM, VM, VM, VM] + [HBM] * len(more),
+        functools.partial(final_kernel, parts),
+        in_specs=[VM, VM] + [VM] * len(parts) + [HBM] * len(more),
         out_specs=HBM,
         out_shape=jax.ShapeDtypeStruct(serving.shape, BF16),
-        input_output_aliases={6: 0} if more else {},
+        input_output_aliases={2 + len(parts): 0} if more else {},
         scratch_shapes=[
-            pltpu.VMEM((2, slots, rows, CHUNK), BF16),
-            pltpu.SemaphoreType.DMA((2, slots * (rows // TILE))),
+            pltpu.VMEM((len(parts), slots, rows, CHUNK), BF16),
+            pltpu.SemaphoreType.DMA((len(parts), slots * (rows // TILE))),
         ],
         compiler_params=pltpu.CompilerParams(vmem_limit_bytes=6 << 20),
         cost_estimate=pl.CostEstimate(
-            flops=serving.size * RANK // 2, bytes_accessed=serving.size, transcendentals=0
+            flops=serving.size * RANK // 4 * len(parts),
+            bytes_accessed=serving.size // 2 * len(parts),
+            transcendentals=0,
         ),
         name="final",
-    )(table, place, y, mine, other, serving, *more)
+    )(y, serving, *tiles, *more)
 
 
 def local(deltas, sketch_matrix, owner_of, serving):
-    c = lax.axis_index("c").astype(jnp.int32).reshape(1)
-    place = jnp.stack([lax.axis_index(a) for a in ("c", "x", "y", "z")]).astype(jnp.int32)
     delta_rows = deltas[0]
     rows = delta_rows.shape[0]
-    mine, other = first_pass(c, delta_rows, sketch_matrix)
+    mine, other = first_pass(delta_rows, sketch_matrix)
     for _ in range(POWER - 1):
         steps = all_sum(mine, other)
-        mine, other = power_pass(power_kernel, c, delta_rows, steps, [], [])
+        mine, other = power_pass(power_kernel, delta_rows, steps, [], [])
     steps = all_sum(mine, other)
     sketch, mine, other, gram_mine, gram_other = power_pass(
         last_kernel,
-        c,
         delta_rows,
         steps,
         [jax.ShapeDtypeStruct((rows, RANK), BF16)],
@@ -447,20 +473,27 @@
     sums = jnp.sum(pieces.astype(F32), axis=0)
     cross = sums[:RANK]
     gram_half = sums[RANK:, :HALF] + sums[RANK:, HALF:]
-    tiles, table = solve(
-        place, owner_of, gram_half, lax.ppermute(gram_half, "c", SWAP), cross
-    )
-    tiles = lax.all_to_all(tiles, "x", 0, 0, tiled=True)
-    tiles = lax.all_to_all(send(table, tiles), "y", 0, 0, tiled=True)
+    solved, table = solve(
+        owner_of, gram_half, lax.ppermute(gram_half, "c", SWAP), cross
+    )
+    tiles = [solved] + [
+        lax.ppermute(solved, "x", [(x, (x + step) % 4) for x in range(4)]) for step in range(1, 4)
+    ]
+    tiles = list(send(table, tiles))
+    for step in range(1, 4):
+        tiles[step] = lax.ppermute(tiles[step], "y", [(y, (y + step) % 4) for y in range(4)])
     tile, y = keep(table, tiles, y_all)
     serving = pltpu.with_memory_space_constraint(serving, pltpu.VMEM)
-    moved = {0: tile}
+    held = {(0, False): tile}
     updated = None
     for step in STEPS[1:]:
-        moved[step] = lax.ppermute(tile, "z", [((z + step) % 4, z) for z in range(4)])
+        held[step, False] = lax.ppermute(
+            tile, "z", [((z + step) % 4, z) for z in range(4)]
+        )
     for step in STEPS:
-        other = lax.ppermute(moved[step], "c", SWAP)
-        updated = final(step, table, place, y, moved[step], other, serving, updated)
+        held[step, True] = lax.ppermute(held[step, False], "c", SWAP)
+    for parts in STAGES:
+        updated = final(parts, [held[part] for part in parts], y, serving, updated)
     return updated
 
 

time: 191 us -> 191 us (level)
  blocking collectives: 89.3 us -> 61 us
  waiting for transfers between devices: 22.5 us -> 44.6 us
  starting transfers between devices: 27.4 us -> 33.4 us
    ppermute x4 -> x10, waiting for transfers between devices: 0.01 us -> 32.6 us  [the longest x3 22.3 us: local(): lax.ppermute(tiles[step], 'y', [(y, (y + step) % 4) for y in range(4)])]
    all_to_all x2 -> x1, blocking collectives: 43.2 us -> 14.9 us  [local(): pieces = lax.all_to_all(packed, 'z', 0, 0, tiled=True)]
    all_to_all x1 -> x0, waiting for transfers between devices: 12.3 us -> none  [local(): pieces = lax.all_to_all(packed, 'z', 0, 0, tiled=True)]
    ppermute x4 -> x10, starting transfers between devices: 10.8 us -> 20.1 us  [the longest x4 10.1 us: local(): held[step, True] = lax.ppermute(held[step, False], 'c', SWAP)]
    all_to_all x1 -> x0, starting transfers between devices: 3.5 us -> none  [local(): pieces = lax.all_to_all(packed, 'z', 0, 0, tiled=True)]
    pallas_call x10 -> x12, Pallas kernels: 35.9 us -> 36 us  [the longest x6 10.7 us: final(): pl.pallas_call(functools.partial(final_kernel, parts), in_specs=[VM, VM]...]
  transfers between devices with their start and end apart: 16 -> 21, of which waited for: 8 -> 14; matrix products, arithmetic and copies ran while one was open for 1% -> 0% of each run, Pallas kernels for 10% -> 10%
where the time goes in v3:
time: 191 us
  blocking collectives  61 us (32%)
  waiting for transfers between devices  44.6 us (23%)
  Pallas kernels  36 us (19%)
  starting transfers between devices  33.4 us (17%)
  between operations  13.7 us (7%)
    all_to_all x2, blocking collectives, all_sum(): pieces = lax.all_to_all(chip, 'z', 0, 0, tiled=True)  25.2 us
    ppermute x3, waiting for transfers between devices, local(): lax.ppermute(tiles[step], 'y', [(y, (y + step) % 4) for y in range(4)])  22.3 us
    all_to_all x2, blocking collectives, all_sum(): lax.all_to_all(jnp.broadcast_to(step[None], (4,) + step.shape), 'z', 0, 0...  20.9 us
    all_to_all x1, blocking collectives, local(): pieces = lax.all_to_all(packed, 'z', 0, 0, tiled=True)  14.9 us
    pallas_call x6, Pallas kernels, final(): pl.pallas_call(functools.partial(final_kernel, parts), in_specs=[VM, VM]...  10.7 us
    pallas_call x1, Pallas kernels, solve(): pl.pallas_call(solve_kernel, in_specs=[SM, VM, VM, VM], out_specs=[VM, SM...  10.6 us
    ppermute x3, waiting for transfers between devices, local(): lax.ppermute(solved, 'x', [(x, (x + step) % 4) for x in range(4)])  10.3 us
    ppermute x4, starting transfers between devices, local(): held[step, True] = lax.ppermute(held[step, False], 'c', SWAP)  10.1 us
  transfers between devices with their start and end apart: 21, of which 14 were waited for; matrix products, arithmetic and copies ran while one was open for 0% of the time, Pallas kernels for 10%

profile of v3, /device:TPU:1, one launch (start us, length us, event | category | flops | bytes accessed | tf_op | source)
XLA Modules:
  0.0 191.1 jit_solution(4262351867324011479)
XLA Ops:
  6.5 5.8 %first.1 = (f32[4,256,256]{2,1,0:T(8,128)S(1)}, bf16[4,256,256]{2,1,0:T(8,128)(2,1)S(1)}) custom-call(bf16[896,2048]{1,0:T(8,128)(2,1)} %bitcast.4, bf16[2048,256]{1,0:T(8,128)(2,1)} %sketch_hbm.1), custom_call_target="tpu_custom_call" | custom-call | tf_op jit(solution)/shard_map/first/pallas_call | solution.py:127
  15.4 13.6 %all_to_all.25 = bf16[4,256,256]{2,1,0:T(8,128)(2,1)S(1)} all-to-all(bf16[4,256,256]{2,1,0:T(8,128)(2,1)S(1)} %add_convert_fusion.2), channel_id=1, replica_groups=mesh['z'=4,'c'=2,'x'=4,'y'=4] {'z'}, dimensions={0} | all-to-all | bytes 1048576 | tf_op jit(solution)/shard_map/all_to_all | solution.py:380
  29.1 10.2 %all_to_all.26.mine_ref = bf16[4,256,256]{2,1,0:T(8,128)(2,1)S(1)} all-to-all(bf16[4,256,256]{2,1,0:T(8,128)(2,1)S(1)} %broadcast_in_dim.6), channel_id=1, replica_groups=mesh['z'=4,'c'=2,'x'=4,'y'=4] {'z'}, dimensions={0} | all-to-all | bytes 1048576 | tf_op jit(solution)/shard_map/all_to_all | solution.py:382
  39.3 2.7 %collective-permute-start.1 = (bf16[4,256,256]{2,1,0:T(8,128)(2,1)S(1)}, bf16[4,256,256]{2,1,0:T(8,128)(2,1)S(1)}, u32[]{:S(2)}, u32[]{:S(2)}) collective-permute-start(bf16[4,256,256]{2,1,0:T(8,128)(2,1)S(1)} %all_to_all.26.mine_ref), channel_id=1, source_target_pairs={{0,16},{16,0},{1,17},{17,1},{2,18},{18,2},{3,19},{19,3},{4,20},{20... | collective-permute-start | bytes 1572872 | tf_op jit(solution)/shard_map/ppermute | solution.py:385
  43.5 2.8 %shard_map.46 = (f32[4,256,256]{2,1,0:T(8,128)S(1)}, bf16[4,256,256]{2,1,0:T(8,128)(2,1)S(1)}) custom-call(bf16[896,2048]{1,0:T(8,128)(2,1)S(1)} %bitcast.5, bf16[4,256,256]{2,1,0:T(8,128)(2,1)S(1)} %all_to_all.26.mine_ref, bf16[4,256,256]{2,1,0:T(8,128)(2,1)S(1)} %collective-permute-done.1.other_ref), custom_call_target="tpu_custom_call" | custom-call | tf_op jit(solution)/shard_map/pallas_call | solution.py:154
  48.4 11.6 %all_to_all.27 = bf16[4,256,256]{2,1,0:T(8,128)(2,1)S(1)} all-to-all(bf16[4,256,256]{2,1,0:T(8,128)(2,1)S(1)} %add_convert_fusion.1), channel_id=1, replica_groups=mesh['z'=4,'c'=2,'x'=4,'y'=4] {'z'}, dimensions={0} | all-to-all | bytes 1048576 | tf_op jit(solution)/shard_map/all_to_all | solution.py:380
  60.2 10.7 %all_to_all.28.mine_ref = bf16[4,256,256]{2,1,0:T(8,128)(2,1)S(1)} all-to-all(bf16[4,256,256]{2,1,0:T(8,128)(2,1)S(1)} %broadcast_in_dim.7), channel_id=1, replica_groups=mesh['z'=4,'c'=2,'x'=4,'y'=4] {'z'}, dimensions={0} | all-to-all | bytes 1048576 | tf_op jit(solution)/shard_map/all_to_all | solution.py:382
  70.9 2.1 %collective-permute-start.3 = (bf16[4,256,256]{2,1,0:T(8,128)(2,1)S(1)}, bf16[4,256,256]{2,1,0:T(8,128)(2,1)S(1)}, u32[]{:S(2)}, u32[]{:S(2)}) collective-permute-start(bf16[4,256,256]{2,1,0:T(8,128)(2,1)S(1)} %all_to_all.28.mine_ref), channel_id=1, source_target_pairs={{0,16},{16,0},{1,17},{17,1},{2,18},{18,2},{3,19},{19,3},{4,20},{20... | collective-permute-start | bytes 1572872 | tf_op jit(solution)/shard_map/ppermute | solution.py:385
  74.5 3.7 %shard_map.47 = (bf16[896,256]{1,0:T(8,128)(2,1)}, f32[4,256,256]{2,1,0:T(8,128)S(1)}, bf16[4,256,256]{2,1,0:T(8,128)(2,1)S(1)}, f32[144,128]{1,0:T(8,128)S(1)}, f32[144,128]{1,0:T(8,128)S(1)}) custom-call(bf16[896,2048]{1,0:T(8,128)(2,1)S(1)} %bitcast.6, bf16[4,256,256]{2,1,0:T(8,128)(2,1)S(1)} %all_to_all.28.mine_ref, ...), custom_call_target="tpu_custom_call" | custom-call | tf_op jit(solution)/shard_map/pallas_call | solution.py:154
  80.7 14.9 %all_to_all.29 = bf16[4,400,256]{2,1,0:T(8,128)(2,1)S(1)} all-to-all(bf16[4,400,256]{2,1,0:T(8,128)(2,1)S(1)} %pad_maximum_fusion), channel_id=1, replica_groups=mesh['z'=4,'c'=2,'x'=4,'y'=4] {'z'}, dimensions={0} | all-to-all | bytes 1638400 | tf_op jit(solution)/shard_map/all_to_all | solution.py:472
  98.2 10.6 %solve.1 = (bf16[256,256]{1,0:T(8,128)(2,1)S(1)}, s32[16]{0:T(128)S(1)}) custom-call(s32[16]{0:T(128)S(1)} %copy-done.2, f32[144,128]{1,0:T(8,128)S(1)} %slice_add_fusion.mine_ref, f32[144,128]{1,0:T(8,128)S(1)} %collective-permute-done.6.other_ref, f32[256,256]{1,0:T(8,128)S(1)} %slice.14.cross_ref), custom_call_target="tpu_custom_call" | custom-call | tf_op jit(solution)/shard_map/solve/pallas_call | solution.py:278
  110.1 2.4 %collective-permute-start.8 = (bf16[256,256]{1,0:T(8,128)(2,1)S(1)}, bf16[256,256]{1,0:T(8,128)(2,1)S(1)}, u32[]{:S(2)}, u32[]{:S(2)}) collective-permute-start(bf16[256,256]{1,0:T(8,128)(2,1)S(1)} %get-tuple-element.31.refs_0_), channel_id=1, source_target_pairs={{0,8},{4,12},{8,0},{12,4},{1,9},{5,13},{9,1},{13,5},{2,10},{6,14},... | collective-permute-start | bytes 393224 | tf_op jit(solution)/shard_map/ppermute | solution.py:480
  113.7 2.1 %collective-permute-done.7.refs_1_ = bf16[256,256]{1,0:T(8,128)(2,1)S(1)} collective-permute-done((bf16[256,256]{1,0:T(8,128)(2,1)S(1)}, bf16[256,256]{1,0:T(8,128)(2,1)S(1)}, u32[]{:S(2)}, u32[]{:S(2)}) %collective-permute-start.7) | collective-permute-done | bytes 131104 | tf_op jit(solution)/shard_map/ppermute | solution.py:480
  115.8 7.7 %collective-permute-done.8.refs_2_ = bf16[256,256]{1,0:T(8,128)(2,1)S(1)} collective-permute-done((bf16[256,256]{1,0:T(8,128)(2,1)S(1)}, bf16[256,256]{1,0:T(8,128)(2,1)S(1)}, u32[]{:S(2)}, u32[]{:S(2)}) %collective-permute-start.8) | collective-permute-done | bytes 131104 | tf_op jit(solution)/shard_map/ppermute | solution.py:480
  126.7 2.8 %collective-permute-start.11 = (bf16[2,256,256]{2,1,0:T(8,128)(2,1)S(1)}, bf16[2,256,256]{2,1,0:T(8,128)(2,1)S(1)}, u32[]{:S(2)}, u32[]{:S(2)}) collective-permute-start(bf16[2,256,256]{2,1,0:T(8,128)(2,1)S(1)} %get-tuple-element.34), channel_id=1, source_target_pairs={{0,2},{1,3},{2,0},{3,1},{4,6},{5,7},{6,4},{7,5},{8,10},{9,11},{10,... | collective-permute-start | bytes 786440 | tf_op jit(solution)/shard_map/ppermute | solution.py:484
  130.4 10.0 %collective-permute-done.10.refs_1_ = bf16[2,256,256]{2,1,0:T(8,128)(2,1)S(1)} collective-permute-done((bf16[2,256,256]{2,1,0:T(8,128)(2,1)S(1)}, bf16[2,256,256]{2,1,0:T(8,128)(2,1)S(1)}, u32[]{:S(2)}, u32[]{:S(2)}) %collective-permute-start.10) | collective-permute-done | bytes 262176 | tf_op jit(solution)/shard_map/ppermute | solution.py:484
  140.4 12.3 %collective-permute-done.11.refs_2_ = bf16[2,256,256]{2,1,0:T(8,128)(2,1)S(1)} collective-permute-done((bf16[2,256,256]{2,1,0:T(8,128)(2,1)S(1)}, bf16[2,256,256]{2,1,0:T(8,128)(2,1)S(1)}, u32[]{:S(2)}, u32[]{:S(2)}) %collective-permute-start.11) | collective-permute-done | bytes 262176 | tf_op jit(solution)/shard_map/ppermute | solution.py:484
  154.6 1.9 keep.1
  162.7 2.1 %collective-permute-done.17.refs_0_ = bf16[2,256,256]{2,1,0:T(8,128)(2,1)S(1)} collective-permute-done((bf16[2,256,256]{2,1,0:T(8,128)(2,1)S(1)}, bf16[2,256,256]{2,1,0:T(8,128)(2,1)S(1)}, u32[]{:S(2)}, u32[]{:S(2)}) %collective-permute-start.17) | collective-permute-done | bytes 262176 | tf_op jit(solution)/shard_map/ppermute | solution.py:490
  164.8 1.9 collective-permute-start.18
  166.7 4.9 %collective-permute-start.16 = (bf16[2,256,256]{2,1,0:T(8,128)(2,1)S(1)}, bf16[2,256,256]{2,1,0:T(8,128)(2,1)S(1)}, u32[]{:S(2)}, u32[]{:S(2)}) collective-permute-start(bf16[2,256,256]{2,1,0:T(8,128)(2,1)S(1)} %collective-permute-done.15.refs_0_), channel_id=1, source_target_pairs={{0,16},{16,0},{1,17},{17,1},{2,18},{18,2},{3,19},{19,3},{4,20},{20... | collective-permute-start | bytes 786440 | tf_op jit(solution)/shard_map/ppermute | solution.py:494
  171.7 1.7 collective-permute-start.14
  173.4 2.1 %final.6.refs_1_ = bf16[2,896,2048]{2,1,0:T(8,128)(2,1)} custom-call(bf16[2,896,256]{2,1,0:T(8,128)(2,1)S(1)} %get-tuple-element.37.y_ref, bf16[2,896,2048]{2,1,0:T(8,128)(2,1)S(1)} %bitcast.3, bf16[2,256,256]{2,1,0:T(8,128)(2,1)S(1)} %get-tuple-element.38.refs_0_, bf16[2,256,256]{2,1,0:T(8,128)(2,1)S(1)} %collective-permute-done.19.refs_1_), custom_call_target="tpu_custom_call" | custom-call | flops 469762048 | bytes 3670016 | tf_op jit(solution)/shard_map/final/pallas_call | solution.py:427
  180.5 2.1 %final.10.refs_1_ = bf16[2,896,2048]{2,1,0:T(8,128)(2,1)} custom-call(bf16[2,896,256]{2,1,0:T(8,128)(2,1)S(1)} %get-tuple-element.37.y_ref, bf16[2,896,2048]{2,1,0:T(8,128)(2,1)S(1)} %bitcast.3, bf16[2,256,256]{2,1,0:T(8,128)(2,1)S(1)} %collective-permute-done.16.refs_0_, ...), custom_call_target="tpu_custom_call", output_to_operand_aliasing={{}: (4, {})} | custom-call | flops 469762048 | bytes 3670016 | tf_op jit(solution)/shard_map/final/pallas_call | solution.py:427
  (67 shorter events, 35.0 us)
Async XLA Ops:
  6.5 148.1 %all-gather.3.cloned.1.call-start = ((), (), s32[]{:S(2)}) async-start(), calls=%async_computation.5 | async-start | bytes 7798784 | tf_op jit(solution)/shard_map/all_gather | solution.py:462
  6.5 37.0 %copy-start = (bf16[1,896,2048]{2,1,0:T(8,128)(2,1)S(1)}, bf16[1,896,2048]{2,1,0:T(8,128)(2,1)}, u32[]{:S(2)}) copy-start(bf16[1,896,2048]{2,1,0:T(8,128)(2,1)} %param.4) | copy-start | bytes 11010052
  12.3 3.0 %collective-permute-start = (bf16[4,256,256]{2,1,0:T(8,128)(2,1)S(1)}, bf16[4,256,256]{2,1,0:T(8,128)(2,1)S(1)}, u32[]{:S(2)}, u32[]{:S(2)}) collective-permute-start(bf16[4,256,256]{2,1,0:T(8,128)(2,1)S(1)} %get-tuple-element.23), channel_id=1, source_target_pairs={{0,16},{16,0},{1,17},{17,1},{2,18},{18,2},{3,19},{19,3},{4,20},{20... | collective-permute-start | bytes 1572872 | tf_op jit(solution)/shard_map/ppermute | solution.py:375
  39.3 4.2 %collective-permute-start.1 = (bf16[4,256,256]{2,1,0:T(8,128)(2,1)S(1)}, bf16[4,256,256]{2,1,0:T(8,128)(2,1)S(1)}, u32[]{:S(2)}, u32[]{:S(2)}) collective-permute-start(bf16[4,256,256]{2,1,0:T(8,128)(2,1)S(1)} %all_to_all.26.mine_ref), channel_id=1, source_target_pairs={{0,16},{16,0},{1,17},{17,1},{2,18},{18,2},{3,19},{19,3},{4,20},{20... | collective-permute-start | bytes 1572872 | tf_op jit(solution)/shard_map/ppermute | solution.py:385
  46.3 2.0 %collective-permute-start.2 = (bf16[4,256,256]{2,1,0:T(8,128)(2,1)S(1)}, bf16[4,256,256]{2,1,0:T(8,128)(2,1)S(1)}, u32[]{:S(2)}, u32[]{:S(2)}) collective-permute-start(bf16[4,256,256]{2,1,0:T(8,128)(2,1)S(1)} %get-tuple-element.25), channel_id=1, source_target_pairs={{0,16},{16,0},{1,17},{17,1},{2,18},{18,2},{3,19},{19,3},{4,20},{20... | collective-permute-start | bytes 1572872 | tf_op jit(solution)/shard_map/ppermute | solution.py:375
  60.1 38.1 %copy-start.2 = (s32[16]{0:T(128)S(1)}, s32[16]{0:T(128)}, u32[]{:S(2)}) copy-start(s32[16]{0:T(128)} %owner_ref.1) | copy-start | bytes 196
  70.9 3.6 %collective-permute-start.3 = (bf16[4,256,256]{2,1,0:T(8,128)(2,1)S(1)}, bf16[4,256,256]{2,1,0:T(8,128)(2,1)S(1)}, u32[]{:S(2)}, u32[]{:S(2)}) collective-permute-start(bf16[4,256,256]{2,1,0:T(8,128)(2,1)S(1)} %all_to_all.28.mine_ref), channel_id=1, source_target_pairs={{0,16},{16,0},{1,17},{17,1},{2,18},{18,2},{3,19},{19,3},{4,20},{20... | collective-permute-start | bytes 1572872 | tf_op jit(solution)/shard_map/ppermute | solution.py:385
  78.3 2.1 %collective-permute-start.4 = (bf16[4,256,256]{2,1,0:T(8,128)(2,1)S(1)}, bf16[4,256,256]{2,1,0:T(8,128)(2,1)S(1)}, u32[]{:S(2)}, u32[]{:S(2)}) collective-permute-start(bf16[4,256,256]{2,1,0:T(8,128)(2,1)S(1)} %get-tuple-element.27), channel_id=1, source_target_pairs={{0,16},{16,0},{1,17},{17,1},{2,18},{18,2},{3,19},{19,3},{4,20},{20... | collective-permute-start | bytes 1572872 | tf_op jit(solution)/shard_map/ppermute | solution.py:375
  78.7 1.6 collective-permute-start.5
  80.6 92.8 %slice-start = ((s8[7340032]{0:T(1024)(128)(4,1)}), s8[3145728]{0:T(1024)(128)(4,1)S(1)}, s32[]{:S(2)}) async-start(s8[7340032]{0:T(1024)(128)(4,1)} %bitcast.2), calls=%async_computation.6 | async-start | bytes 6291456
  95.7 2.5 %collective-permute-start.6 = (f32[144,128]{1,0:T(8,128)S(1)}, f32[144,128]{1,0:T(8,128)S(1)}, u32[]{:S(2)}, u32[]{:S(2)}) collective-permute-start(f32[144,128]{1,0:T(8,128)S(1)} %slice_add_fusion.mine_ref), channel_id=1, source_target_pairs={{0,16},{16,0},{1,17},{17,1},{2,18},{18,2},{3,19},{19,3},{4,20},{20... | collective-permute-start | bytes 221192 | tf_op jit(solution)/shard_map/ppermute | solution.py:477
  108.8 7.0 %collective-permute-start.7 = (bf16[256,256]{1,0:T(8,128)(2,1)S(1)}, bf16[256,256]{1,0:T(8,128)(2,1)S(1)}, u32[]{:S(2)}, u32[]{:S(2)}) collective-permute-start(bf16[256,256]{1,0:T(8,128)(2,1)S(1)} %get-tuple-element.31.refs_0_), channel_id=1, source_target_pairs={{0,4},{4,8},{8,12},{12,0},{1,5},{5,9},{9,13},{13,1},{2,6},{6,10},{... | collective-permute-start | bytes 393224 | tf_op jit(solution)/shard_map/ppermute | solution.py:480
  110.1 13.4 %collective-permute-start.8 = (bf16[256,256]{1,0:T(8,128)(2,1)S(1)}, bf16[256,256]{1,0:T(8,128)(2,1)S(1)}, u32[]{:S(2)}, u32[]{:S(2)}) collective-permute-start(bf16[256,256]{1,0:T(8,128)(2,1)S(1)} %get-tuple-element.31.refs_0_), channel_id=1, source_target_pairs={{0,8},{4,12},{8,0},{12,4},{1,9},{5,13},{9,1},{13,5},{2,10},{6,14},... | collective-permute-start | bytes 393224 | tf_op jit(solution)/shard_map/ppermute | solution.py:480
  112.5 11.5 %collective-permute-start.9 = (bf16[256,256]{1,0:T(8,128)(2,1)S(1)}, bf16[256,256]{1,0:T(8,128)(2,1)S(1)}, u32[]{:S(2)}, u32[]{:S(2)}) collective-permute-start(bf16[256,256]{1,0:T(8,128)(2,1)S(1)} %get-tuple-element.31.refs_0_), channel_id=1, source_target_pairs={{0,12},{4,0},{8,4},{12,8},{1,13},{5,1},{9,5},{13,9},{2,14},{6,2},{... | collective-permute-start | bytes 393224 | tf_op jit(solution)/shard_map/ppermute | solution.py:480
  125.4 15.0 %collective-permute-start.10 = (bf16[2,256,256]{2,1,0:T(8,128)(2,1)S(1)}, bf16[2,256,256]{2,1,0:T(8,128)(2,1)S(1)}, u32[]{:S(2)}, u32[]{:S(2)}) collective-permute-start(bf16[2,256,256]{2,1,0:T(8,128)(2,1)S(1)} %get-tuple-element.33), channel_id=1, source_target_pairs={{0,1},{1,2},{2,3},{3,0},{4,5},{5,6},{6,7},{7,4},{8,9},{9,10},{10,1... | collective-permute-start | bytes 786440 | tf_op jit(solution)/shard_map/ppermute | solution.py:484
  126.7 26.0 %collective-permute-start.11 = (bf16[2,256,256]{2,1,0:T(8,128)(2,1)S(1)}, bf16[2,256,256]{2,1,0:T(8,128)(2,1)S(1)}, u32[]{:S(2)}, u32[]{:S(2)}) collective-permute-start(bf16[2,256,256]{2,1,0:T(8,128)(2,1)S(1)} %get-tuple-element.34), channel_id=1, source_target_pairs={{0,2},{1,3},{2,0},{3,1},{4,6},{5,7},{6,4},{7,5},{8,10},{9,11},{10,... | collective-permute-start | bytes 786440 | tf_op jit(solution)/shard_map/ppermute | solution.py:484
  129.5 24.0 %collective-permute-start.12 = (bf16[2,256,256]{2,1,0:T(8,128)(2,1)S(1)}, bf16[2,256,256]{2,1,0:T(8,128)(2,1)}, u32[]{:S(2)}, u32[]{:S(2)}) collective-permute-start(bf16[2,256,256]{2,1,0:T(8,128)(2,1)S(1)} %get-tuple-element.35), channel_id=1, source_target_pairs={{0,3},{1,0},{2,1},{3,2},{4,7},{5,4},{6,5},{7,6},{8,11},{9,8},{10,9... | collective-permute-start | bytes 786440 | tf_op jit(solution)/shard_map/ppermute | solution.py:484
  156.5 8.3 %collective-permute-start.17 = (bf16[2,256,256]{2,1,0:T(8,128)(2,1)S(1)}, bf16[2,256,256]{2,1,0:T(8,128)(2,1)S(1)}, u32[]{:S(2)}, u32[]{:S(2)}) collective-permute-start(bf16[2,256,256]{2,1,0:T(8,128)(2,1)S(1)} %get-tuple-element.38.refs_0_), channel_id=1, source_target_pairs={{96,0},{0,32},{32,64},{64,96},{97,1},{1,33},{33,65},{65,97},{98,2}... | collective-permute-start | bytes 786440 | tf_op jit(solution)/shard_map/ppermute | solution.py:490
  158.0 8.8 %collective-permute-start.15 = (bf16[2,256,256]{2,1,0:T(8,128)(2,1)S(1)}, bf16[2,256,256]{2,1,0:T(8,128)(2,1)S(1)}, u32[]{:S(2)}, u32[]{:S(2)}) collective-permute-start(bf16[2,256,256]{2,1,0:T(8,128)(2,1)S(1)} %get-tuple-element.38.refs_0_), channel_id=1, source_target_pairs={{32,0},{64,32},{96,64},{0,96},{33,1},{65,33},{97,65},{1,97},{34,2}... | collective-permute-start | bytes 786440 | tf_op jit(solution)/shard_map/ppermute | solution.py:490
  159.4 12.3 %collective-permute-start.13 = (bf16[2,256,256]{2,1,0:T(8,128)(2,1)S(1)}, bf16[2,256,256]{2,1,0:T(8,128)(2,1)S(1)}, u32[]{:S(2)}, u32[]{:S(2)}) collective-permute-start(bf16[2,256,256]{2,1,0:T(8,128)(2,1)S(1)} %get-tuple-element.38.refs_0_), channel_id=1, source_target_pairs={{64,0},{96,32},{0,64},{32,96},{65,1},{97,33},{1,65},{33,97},{66,2}... | collective-permute-start | bytes 786440 | tf_op jit(solution)/shard_map/ppermute | solution.py:490
  161.0 12.4 %collective-permute-start.19 = (bf16[2,256,256]{2,1,0:T(8,128)(2,1)S(1)}, bf16[2,256,256]{2,1,0:T(8,128)(2,1)S(1)}, u32[]{:S(2)}, u32[]{:S(2)}) collective-permute-start(bf16[2,256,256]{2,1,0:T(8,128)(2,1)S(1)} %get-tuple-element.38.refs_0_), channel_id=1, source_target_pairs={{0,16},{16,0},{1,17},{17,1},{2,18},{18,2},{3,19},{19,3},{4,20},{20... | collective-permute-start | bytes 786440 | tf_op jit(solution)/shard_map/ppermute | solution.py:494
  164.8 12.3 %collective-permute-start.18 = (bf16[2,256,256]{2,1,0:T(8,128)(2,1)S(1)}, bf16[2,256,256]{2,1,0:T(8,128)(2,1)S(1)}, u32[]{:S(2)}, u32[]{:S(2)}) collective-permute-start(bf16[2,256,256]{2,1,0:T(8,128)(2,1)S(1)} %collective-permute-done.17.refs_0_), channel_id=1, source_target_pairs={{0,16},{16,0},{1,17},{17,1},{2,18},{18,2},{3,19},{19,3},{4,20},{20... | collective-permute-start | bytes 786440 | tf_op jit(solution)/shard_map/ppermute | solution.py:494
  166.7 13.7 %collective-permute-start.16 = (bf16[2,256,256]{2,1,0:T(8,128)(2,1)S(1)}, bf16[2,256,256]{2,1,0:T(8,128)(2,1)S(1)}, u32[]{:S(2)}, u32[]{:S(2)}) collective-permute-start(bf16[2,256,256]{2,1,0:T(8,128)(2,1)S(1)} %collective-permute-done.15.refs_0_), channel_id=1, source_target_pairs={{0,16},{16,0},{1,17},{17,1},{2,18},{18,2},{3,19},{19,3},{4,20},{20... | collective-permute-start | bytes 786440 | tf_op jit(solution)/shard_map/ppermute | solution.py:494
  171.7 10.8 %collective-permute-start.14 = (bf16[2,256,256]{2,1,0:T(8,128)(2,1)S(1)}, bf16[2,256,256]{2,1,0:T(8,128)(2,1)S(1)}, u32[]{:S(2)}, u32[]{:S(2)}) collective-permute-start(bf16[2,256,256]{2,1,0:T(8,128)(2,1)S(1)} %collective-permute-done.13.refs_1_), channel_id=1, source_target_pairs={{0,16},{16,0},{1,17},{17,1},{2,18},{18,2},{3,19},{19,3},{4,20},{20... | collective-permute-start | bytes 786440 | tf_op jit(solution)/shard_map/ppermute | solution.py:494
  (4 other events, 34.4 us)
Sparse Core Ops, SparseCore 0:
  78.4 76.1 all-gather.2
